TPU v7x, 32 devices: a whole 2x2x4 slice. The times are simulated.
32 devices in a mesh: dp: 8 (over z, x), tensor: 4 (over y, core).
Axes of the slice: x: 2, y: 2, z: 4, core: 2. Of those that a mesh axis runs over, the one named last changes fastest.
Arguments:
- doc_hidden: bfloat16 [4096, 1024], P(('dp', 'tensor')), may hold values from -6 to 6
- query_hidden: bfloat16 [1024, 1024], P(('dp', 'tensor')), may hold values from -6 to 6
- seg_lengths: int32 [8, 4], P('dp'), may hold values from 16 to 128, as said below
- labels: int32 [32], P(('dp', 'tensor')), may hold values from 0 to 31
- w_qkv: bfloat16 [2, 1024, 3, 1024], P(None, None, None, 'tensor'), may hold values from -0.1875 to 0.1875
- b_qkv: float32 [2, 3, 1024], P(None, None, 'tensor'), may hold values from -1.8 to 1.8
- w_attn_out: bfloat16 [2, 1024, 1024], P(None, 'tensor'), may hold values from -1.5 to 1.5
- w_ff_in: bfloat16 [2, 1024, 4096], P(None, None, 'tensor'), may hold values from -0.1875 to 0.1875
- b_ff_in: float32 [2, 4096], P(None, 'tensor'), may hold values from -1.8 to 1.8
- w_ff_out: bfloat16 [2, 4096, 1024], P(None, 'tensor'), may hold values from -0.1875 to 0.1875
- out_bias: float32 [2, 2, 1024], replicated, may hold values from -1.8 to 1.8
- norm_gain: float32 [2, 2, 1024], replicated, may hold values from 0.5 to 1.5
- norm_bias: float32 [2, 2, 1024], replicated, may hold values from -1.2 to 1.2
- w_proj: bfloat16 [1024, 128], replicated, may hold values from -0.1875 to 0.1875
Outputs:
- query_losses: float32 [32], P(('dp', 'tensor'))
- g_doc_hidden: float32 [4096, 1024], P(('dp', 'tensor'))
- g_query_hidden: float32 [1024, 1024], P(('dp', 'tensor'))
- g_w_qkv: float32 [2, 1024, 3, 1024], P(None, 'dp', None, 'tensor')
- g_b_qkv: float32 [2, 3, 1024], P(None, None, ('tensor', 'dp'))
- g_w_attn_out: float32 [2, 1024, 1024], P(None, 'tensor', 'dp')
- g_w_ff_in: float32 [2, 1024, 4096], P(None, 'dp', 'tensor')
- g_b_ff_in: float32 [2, 4096], P(None, ('tensor', 'dp'))
- g_w_ff_out: float32 [2, 4096, 1024], P(None, 'tensor', 'dp')
- g_out_bias: float32 [2, 2, 1024], P(None, None, ('dp', 'tensor'))
- g_norm_gain: float32 [2, 2, 1024], P(None, None, ('dp', 'tensor'))
- g_norm_bias: float32 [2, 2, 1024], P(None, None, ('dp', 'tensor'))
- g_w_proj: float32 [1024, 128], P(('dp', 'tensor'))
Inputs may be any that keep to these rules, and one draw needn't show every extreme that they name: `seg_lengths`: each entry is the length of one document of a row, between 16 and 128; every row has an entry equal to 128; a row's entries sum to at most 512, and the rest of the row is padding.
All inputs are finite; a program needn't handle non-finite values.
Results may differ from a plain program's by a relative error of at most 0.024.
Values may be sent and summed in bfloat16 or wider, within the bound.
No kernel may reach another device: no remote copies, remote signals or barrier semaphores. Data moves between devices by JAX's collectives and lax.ppermute only.
A program may use at most 192 MiB of HBM per device.

v0:
```python
import math

import jax
import jax.numpy as jnp
from jax import lax
from jax.sharding import PartitionSpec as P

HD = 64
LAYERS = 2


precise = lax.Precision.HIGHEST
eps_norm = 1e-05
eps_unit = 1e-06
tau_token = 0.1
temp_loss = 0.1
masked_score = -1000000000.0


def inner(left, right):
    return lax.dot_general(
        left, right, (((0,), (0,)), ((), ())), preferred_element_type=jnp.float32
    )


def times_t(left, right):
    return lax.dot_general(
        left, right, (((1,), (1,)), ((), ())), preferred_element_type=jnp.float32
    )


def inner_exact(left, right):
    return lax.dot_general(
        left, right, (((0,), (0,)), ((), ())), precision=precise, preferred_element_type=jnp.float32
    )


def times_t_exact(left, right):
    return lax.dot_general(
        left, right, (((1,), (1,)), ((), ())), precision=precise, preferred_element_type=jnp.float32
    )


def layer_norm(values, gain_row, bias_row):
    average = jnp.mean(values, axis=-1, keepdims=True)
    centred = values - average
    spread = jnp.mean(centred * centred, axis=-1, keepdims=True)
    return centred * lax.rsqrt(spread + eps_norm) * gain_row + bias_row


def unit(values):
    return values * lax.rsqrt(jnp.sum(values * values, axis=-1, keepdims=True) + eps_unit)


def gelu_exact(values):
    return jax.nn.gelu(values, approximate=False)


def row_layout(lengths, row_len):
    doc_ends = jnp.cumsum(lengths)
    token_idx = jnp.arange(row_len, dtype=jnp.int32)
    passed = (token_idx[:, None] >= doc_ends[None, :]).astype(jnp.int32)
    segment = jnp.sum(passed, axis=1)
    starts = jnp.sum(passed * lengths[None, :], axis=1)
    return (segment, token_idx - starts)


def rotary_tables(positions, head_dim):
    half_dim = head_dim // 2
    frequency = jnp.exp(jnp.arange(half_dim, dtype=jnp.float32) * (-math.log(10000.0) / half_dim))
    angles = positions.astype(jnp.float32)[:, None] * frequency[None, :]
    angles = jnp.concatenate([angles, angles], axis=1)
    return (jnp.cos(angles), jnp.sin(angles))


def rotate(values, cos_table, sine_table):
    half_dim = values.shape[-1] // 2
    turned = jnp.concatenate([-values[..., half_dim:], values[..., :half_dim]], axis=-1)
    return values * cos_table[:, None, :] + turned * sine_table[:, None, :]


def rotate_back(grads, cos_table, sine_table):
    half_dim = grads.shape[-1] // 2
    scaled = grads * sine_table[:, None, :]
    turned = jnp.concatenate([scaled[..., half_dim:], -scaled[..., :half_dim]], axis=-1)
    return grads * cos_table[:, None, :] + turned


def gather_rows(doc_part, query_part):
    return (
        lax.all_gather(doc_part, "tensor", axis=0, tiled=True),
        lax.all_gather(query_part, "tensor", axis=0, tiled=True),
    )


def share_rows(doc_part, query_part):
    return (
        lax.psum_scatter(doc_part, "tensor", scatter_dimension=0, tiled=True),
        lax.psum_scatter(query_part, "tensor", scatter_dimension=0, tiled=True),
    )


def gather_grads(doc_part, query_part):
    return (
        lax.all_gather(doc_part, "tensor", axis=0, tiled=True),
        lax.all_gather(query_part, "tensor", axis=0, tiled=True),
    )


def share_grads(doc_part, query_part):
    return (
        lax.psum_scatter(doc_part, "tensor", scatter_dimension=0, tiled=True),
        lax.psum_scatter(query_part, "tensor", scatter_dimension=0, tiled=True),
    )


def block_scores(block_q, keys, block_seg, segment, scale_qk):
    scores = (
        jnp.einsum("qhd,khd->hqk", block_q, keys, preferred_element_type=jnp.float32) * scale_qk
    )
    return jnp.where((block_seg[:, None] == segment[None, :])[None], scores, masked_score)


def attend_forward(queries, keys, values, segment):
    row_count = queries.shape[0]
    block_len = min(512, row_count)
    scale_qk = queries.shape[2] ** (-0.5)

    def one_block(offset):
        scores = block_scores(queries, keys, segment, segment, scale_qk)
        peak = jnp.max(scores, axis=-1, keepdims=True)
        log_total = peak + jnp.log(jnp.sum(jnp.exp(scores - peak), axis=-1, keepdims=True))
        attn_probs = jnp.exp(scores - log_total).astype(jnp.bfloat16)
        result = jnp.einsum("hqk,khd->qhd", attn_probs, values, preferred_element_type=jnp.float32)
        return (result, log_total[..., 0])

    offsets = jnp.arange(row_count // block_len) * block_len
    results, log_totals = lax.map(one_block, offsets)
    return (results.reshape(queries.shape), log_totals)


def attend_backward(queries, keys, values, segment, log_totals, grad_out):
    row_count = queries.shape[0]
    block_len = min(512, row_count)
    scale_qk = queries.shape[2] ** (-0.5)

    def one_block(carry, index):
        key_grad, value_grad = carry
        scores = block_scores(queries, keys, segment, segment, scale_qk)
        attn_probs = jnp.exp(scores - log_totals[index][..., None])
        prob_grad = jnp.einsum("qhd,khd->hqk", grad_out, values, preferred_element_type=jnp.float32)
        delta_row = jnp.sum(attn_probs * prob_grad, axis=-1, keepdims=True)
        score_grad = (attn_probs * (prob_grad - delta_row)).astype(jnp.bfloat16)
        query_grad = (
            jnp.einsum("hqk,khd->qhd", score_grad, keys, preferred_element_type=jnp.float32)
            * scale_qk
        )
        key_grad = (
            key_grad
            + jnp.einsum("hqk,qhd->khd", score_grad, queries, preferred_element_type=jnp.float32)
            * scale_qk
        )
        value_grad = value_grad + jnp.einsum(
            "hqk,qhd->khd",
            attn_probs.astype(jnp.bfloat16),
            grad_out,
            preferred_element_type=jnp.float32,
        )
        return ((key_grad, value_grad), query_grad)

    zeros = jnp.zeros(keys.shape, jnp.float32)
    block_total = row_count // block_len
    (key_grad, value_grad), query_grads = lax.scan(
        one_block, (zeros, zeros), jnp.arange(block_total, dtype=jnp.int32)
    )
    return (query_grads.reshape(queries.shape), key_grad, value_grad)


def layer_forward(state, share_docs, params, layer_idx, layout):
    w_qkv, b_qkv, w_attn_out, w_ff_in, b_ff_in, w_ff_out, out_bias, norm_gain, norm_bias = params
    doc_segment, query_segment, cos_table, sine_table = layout
    state_low = state.astype(jnp.bfloat16)
    doc_full, query_full = gather_rows(state_low[:share_docs], state_low[share_docs:])
    inputs = jnp.concatenate([doc_full, query_full], axis=0)
    row_count, width = inputs.shape
    doc_rows = doc_full.shape[0]
    local_width = w_qkv.shape[3]
    head_count = local_width // HD
    mixed = jnp.dot(
        inputs, w_qkv[layer_idx].reshape(width, 3 * local_width), preferred_element_type=jnp.float32
    )
    mixed = mixed.reshape(row_count, 3, local_width) + b_qkv[layer_idx][None]
    head_shape = (row_count, head_count, HD)
    queries = rotate(mixed[:, 0].reshape(head_shape), cos_table, sine_table).astype(jnp.bfloat16)
    keys = rotate(mixed[:, 1].reshape(head_shape), cos_table, sine_table).astype(jnp.bfloat16)
    values = mixed[:, 2].reshape(head_shape).astype(jnp.bfloat16)
    doc_out, doc_logs = attend_forward(
        queries[:doc_rows], keys[:doc_rows], values[:doc_rows], doc_segment
    )
    query_out, query_logs = attend_forward(
        queries[doc_rows:], keys[doc_rows:], values[doc_rows:], query_segment
    )
    attended = (
        jnp.concatenate([doc_out, query_out], axis=0)
        .reshape(row_count, local_width)
        .astype(jnp.bfloat16)
    )
    branch_terms = jnp.dot(attended, w_attn_out[layer_idx], preferred_element_type=jnp.float32)
    doc_branch, query_branch = share_rows(branch_terms[:doc_rows], branch_terms[doc_rows:])
    residual = state + jnp.concatenate([doc_branch, query_branch], axis=0) + out_bias[layer_idx, 0]
    normed = layer_norm(residual, norm_gain[layer_idx, 0], norm_bias[layer_idx, 0])
    normed_low = normed.astype(jnp.bfloat16)
    doc_normed, query_normed = gather_rows(normed_low[:share_docs], normed_low[share_docs:])
    normed_full = jnp.concatenate([doc_normed, query_normed], axis=0)
    upward = (
        jnp.dot(normed_full, w_ff_in[layer_idx], preferred_element_type=jnp.float32)
        + b_ff_in[layer_idx]
    )
    activated = gelu_exact(upward).astype(jnp.bfloat16)
    ff_terms = jnp.dot(activated, w_ff_out[layer_idx], preferred_element_type=jnp.float32)
    doc_ff, query_ff = share_rows(ff_terms[:doc_rows], ff_terms[doc_rows:])
    combined = normed + jnp.concatenate([doc_ff, query_ff], axis=0) + out_bias[layer_idx, 1]
    output = layer_norm(combined, norm_gain[layer_idx, 1], norm_bias[layer_idx, 1])
    kept = (
        inputs,
        queries,
        keys,
        values,
        doc_logs,
        query_logs,
        attended,
        residual,
        normed_full,
        upward,
        activated,
        combined,
    )
    return (output, kept)


def layer_backward(grad_state, kept, share_docs, params, layer_idx, layout):
    w_qkv, b_qkv, w_attn_out, w_ff_in, b_ff_in, w_ff_out, out_bias, norm_gain, norm_bias = params
    doc_segment, query_segment, cos_table, sine_table = layout
    (
        inputs,
        queries,
        keys,
        values,
        doc_logs,
        query_logs,
        attended,
        residual,
        normed_full,
        upward,
        activated,
        combined,
    ) = kept
    row_count, width = inputs.shape
    doc_rows = doc_segment.shape[0]
    local_width = w_qkv.shape[3]
    _, norm_pull = jax.vjp(layer_norm, combined, norm_gain[layer_idx, 1], norm_bias[layer_idx, 1])
    g_combined, g_gain_ff, g_shift_ff = norm_pull(grad_state)
    g_branch_ff = g_combined.astype(jnp.bfloat16)
    g_bias_ff = jnp.sum(g_branch_ff, axis=0, dtype=jnp.float32)
    doc_gf, query_gf = gather_grads(g_branch_ff[:share_docs], g_branch_ff[share_docs:])
    g_ff_full = jnp.concatenate([doc_gf, query_gf], axis=0)
    g_ff_out = inner(activated, g_ff_full)
    g_activated = times_t(g_ff_full, w_ff_out[layer_idx])
    _, gelu_pull = jax.vjp(gelu_exact, upward)
    g_upward = gelu_pull(g_activated)[0].astype(jnp.bfloat16)
    g_b_ff_in = jnp.sum(g_upward, axis=0, dtype=jnp.float32)
    g_ff_in = inner(normed_full, g_upward)
    ff_back = times_t(g_upward, w_ff_in[layer_idx])
    doc_back, query_back = share_grads(ff_back[:doc_rows], ff_back[doc_rows:])
    g_normed = g_combined + jnp.concatenate([doc_back, query_back], axis=0)
    _, first_pull = jax.vjp(layer_norm, residual, norm_gain[layer_idx, 0], norm_bias[layer_idx, 0])
    g_residual, g_gain_attn, g_shift_attn = first_pull(g_normed)
    g_branch_attn = g_residual.astype(jnp.bfloat16)
    g_bias_attn = jnp.sum(g_branch_attn, axis=0, dtype=jnp.float32)
    doc_ga, query_ga = gather_grads(g_branch_attn[:share_docs], g_branch_attn[share_docs:])
    g_attn_full = jnp.concatenate([doc_ga, query_ga], axis=0)
    g_attn_out = inner(attended, g_attn_full)
    g_attended = (
        times_t(g_attn_full, w_attn_out[layer_idx]).reshape(queries.shape).astype(jnp.bfloat16)
    )
    doc_gq, doc_gk, doc_gv = attend_backward(
        queries[:doc_rows],
        keys[:doc_rows],
        values[:doc_rows],
        doc_segment,
        doc_logs,
        g_attended[:doc_rows],
    )
    query_gq, query_gk, query_gv = attend_backward(
        queries[doc_rows:],
        keys[doc_rows:],
        values[doc_rows:],
        query_segment,
        query_logs,
        g_attended[doc_rows:],
    )
    g_queries = rotate_back(jnp.concatenate([doc_gq, query_gq], axis=0), cos_table, sine_table)
    g_keys = rotate_back(jnp.concatenate([doc_gk, query_gk], axis=0), cos_table, sine_table)
    g_values = jnp.concatenate([doc_gv, query_gv], axis=0)
    g_mixed = (
        jnp.stack([g_queries, g_keys, g_values], axis=1)
        .reshape(row_count, 3 * local_width)
        .astype(jnp.bfloat16)
    )
    g_b_qkv = jnp.sum(g_mixed, axis=0, dtype=jnp.float32).reshape(3, local_width)
    g_qkv = inner(inputs, g_mixed).reshape(width, 3, local_width)
    in_back = times_t(g_mixed, w_qkv[layer_idx].reshape(width, 3 * local_width))
    doc_in, query_in = share_grads(in_back[:doc_rows], in_back[doc_rows:])
    g_state = g_residual + jnp.concatenate([doc_in, query_in], axis=0)
    weight_grads = (g_qkv, g_b_qkv, g_attn_out, g_ff_in, g_b_ff_in, g_ff_out)
    small_parts = (
        jnp.stack([g_bias_attn, g_bias_ff]),
        jnp.stack([g_gain_attn, g_gain_ff]),
        jnp.stack([g_shift_attn, g_shift_ff]),
    )
    return (g_state, weight_grads, small_parts)


def token_scores(query_vecs, doc_vecs, doc_lens):
    doc_count = doc_lens.shape[0]
    segment, _ = row_layout(doc_lens, doc_vecs.shape[0])
    scaled = times_t_exact(query_vecs, doc_vecs) / tau_token
    log_list = []
    for doc_pos in range(doc_count):
        masked = jnp.where((segment == doc_pos)[None, :], scaled, masked_score)
        peak = jnp.max(masked, axis=1)
        log_list.append(peak + jnp.log(jnp.sum(jnp.exp(masked - peak[:, None]), axis=1)))
    log_sums = jnp.stack(log_list, axis=1)
    return (tau_token * (log_sums - jnp.log(doc_lens.astype(jnp.float32))[None, :]), log_sums)


def token_back(query_vecs, doc_vecs, doc_lens, g_tokens, log_sums):
    doc_count = doc_lens.shape[0]
    segment, _ = row_layout(doc_lens, doc_vecs.shape[0])
    member = (segment[None, :] == jnp.arange(doc_count, dtype=jnp.int32)[:, None]).astype(
        jnp.float32
    )
    scaled = times_t_exact(query_vecs, doc_vecs) / tau_token
    log_spread = jnp.dot(log_sums, member, precision=precise, preferred_element_type=jnp.float32)
    g_spread = jnp.dot(g_tokens, member, precision=precise, preferred_element_type=jnp.float32)
    valid = (segment < doc_count)[None, :]
    g_sims = jnp.where(valid, g_spread * jnp.exp(scaled - log_spread), 0.0)
    return (
        jnp.dot(g_sims, doc_vecs, precision=precise, preferred_element_type=jnp.float32),
        inner_exact(g_sims, query_vecs),
    )


def query_objective(doc_scores, label):
    logits = doc_scores / temp_loss
    peak = jnp.max(logits)
    log_total = peak + jnp.log(jnp.sum(jnp.exp(logits - peak)))
    target = (jnp.arange(logits.shape[0], dtype=jnp.int32) == label).astype(jnp.float32)
    chosen = jnp.sum(target * logits)
    return ((log_total - chosen)[None], (jnp.exp(logits - log_total) - target) / temp_loss)


def per_device(
    doc_hidden,
    query_hidden,
    seg_lengths,
    labels,
    w_qkv,
    b_qkv,
    w_attn_out,
    w_ff_in,
    b_ff_in,
    w_ff_out,
    out_bias,
    norm_gain,
    norm_bias,
    w_proj,
):
    tensor_size = lax.axis_size("tensor")
    share_docs = doc_hidden.shape[0]
    query_len = query_hidden.shape[0]
    row_len = share_docs * tensor_size
    doc_lens = seg_lengths[0]
    doc_count = doc_lens.shape[0]
    doc_segment, doc_position = row_layout(doc_lens, row_len)
    query_place = jnp.arange(query_len * tensor_size, dtype=jnp.int32)
    query_segment = query_place // query_len
    positions = jnp.concatenate([doc_position, query_place % query_len])
    cos_table, sine_table = rotary_tables(positions, HD)
    layout = (doc_segment, query_segment, cos_table, sine_table)
    params = (w_qkv, b_qkv, w_attn_out, w_ff_in, b_ff_in, w_ff_out, out_bias, norm_gain, norm_bias)
    state = jnp.concatenate([doc_hidden, query_hidden], axis=0).astype(jnp.float32)
    kept_all = []
    for layer_idx in range(LAYERS):
        state, kept = layer_forward(state, share_docs, params, layer_idx, layout)
        kept_all.append(kept)
    proj_exact = w_proj.astype(jnp.float32)
    projected = jnp.dot(state, proj_exact, precision=precise, preferred_element_type=jnp.float32)
    vectors = unit(projected)
    doc_vecs = vectors[:share_docs]
    query_vecs = vectors[share_docs:]
    row_full = lax.all_gather(doc_vecs, "tensor", axis=0, tiled=True)
    all_queries = lax.all_gather(query_vecs, "dp", axis=0, tiled=True)
    group_count = all_queries.shape[0] // query_len
    tok_scores, tok_logs = token_scores(all_queries, row_full, doc_lens)
    query_scores = jnp.sum(tok_scores.reshape(group_count, query_len, doc_count), axis=1)
    doc_scores = lax.all_to_all(
        query_scores, "dp", split_axis=0, concat_axis=1, tiled=True
    ).reshape(group_count * doc_count)
    query_loss, g_logits = query_objective(doc_scores, labels[0])
    g_groups = lax.all_to_all(
        g_logits.reshape(1, group_count * doc_count), "dp", split_axis=1, concat_axis=0, tiled=True
    )
    g_tok = jnp.broadcast_to(g_groups[:, None, :], (group_count, query_len, doc_count)).reshape(
        group_count * query_len, doc_count
    )
    g_all_queries, g_row_docs = token_back(all_queries, row_full, doc_lens, g_tok, tok_logs)
    g_doc_vecs = lax.psum_scatter(g_row_docs, "tensor", scatter_dimension=0, tiled=True)
    g_query_vecs = lax.psum_scatter(g_all_queries, "dp", scatter_dimension=0, tiled=True)
    g_vectors = jnp.concatenate([g_doc_vecs, g_query_vecs], axis=0)
    _, unit_pull = jax.vjp(unit, projected)
    g_projected = unit_pull(g_vectors)[0]
    g_w_proj = inner_exact(state, g_projected)
    grad_state = times_t_exact(g_projected, proj_exact)
    layer_reduced = [None] * LAYERS
    small_list = [None] * LAYERS
    for layer_idx in reversed(range(LAYERS)):
        grad_state, weight_grads, small_parts = layer_backward(
            grad_state, kept_all[layer_idx], share_docs, params, layer_idx, layout
        )
        layer_reduced[layer_idx] = (
            lax.psum_scatter(weight_grads[0], "dp", scatter_dimension=0, tiled=True),
            lax.psum_scatter(weight_grads[1], "dp", scatter_dimension=1, tiled=True),
            lax.psum_scatter(weight_grads[2], "dp", scatter_dimension=1, tiled=True),
            lax.psum_scatter(weight_grads[3], "dp", scatter_dimension=0, tiled=True),
            lax.psum_scatter(weight_grads[4], "dp", scatter_dimension=0, tiled=True),
            lax.psum_scatter(weight_grads[5], "dp", scatter_dimension=1, tiled=True),
        )
        small_list[layer_idx] = small_parts
    stacked = tuple(
        (
            jnp.stack([layer_reduced[layer_pos][member_pos] for layer_pos in range(LAYERS)])
            for member_pos in range(6)
        )
    )
    bias_grads = jnp.stack([small_list[layer_pos][0] for layer_pos in range(LAYERS)])
    gain_grads = jnp.stack([small_list[layer_pos][1] for layer_pos in range(LAYERS)])
    shift_grads = jnp.stack([small_list[layer_pos][2] for layer_pos in range(LAYERS)])
    small_reduced = (
        lax.psum_scatter(bias_grads, ("dp", "tensor"), scatter_dimension=2, tiled=True),
        lax.psum_scatter(gain_grads, ("dp", "tensor"), scatter_dimension=2, tiled=True),
        lax.psum_scatter(shift_grads, ("dp", "tensor"), scatter_dimension=2, tiled=True),
        lax.psum_scatter(g_w_proj, ("dp", "tensor"), scatter_dimension=0, tiled=True),
    )
    return (
        query_loss,
        grad_state[:share_docs],
        grad_state[share_docs:],
        stacked[0],
        stacked[1],
        stacked[2],
        stacked[3],
        stacked[4],
        stacked[5],
        small_reduced[0],
        small_reduced[1],
        small_reduced[2],
        small_reduced[3],
    )


def solution(mesh):
    return jax.shard_map(
        per_device,
        mesh=mesh,
        in_specs=(
            P(("dp", "tensor"), None),
            P(("dp", "tensor"), None),
            P("dp", None),
            P(("dp", "tensor")),
            P(None, None, None, "tensor"),
            P(None, None, "tensor"),
            P(None, "tensor", None),
            P(None, None, "tensor"),
            P(None, "tensor"),
            P(None, "tensor", None),
            P(),
            P(),
            P(),
            P(),
        ),
        out_specs=(
            P(("dp", "tensor")),
            P(("dp", "tensor"), None),
            P(("dp", "tensor"), None),
            P(None, "dp", None, "tensor"),
            P(None, None, ("tensor", "dp")),
            P(None, "tensor", "dp"),
            P(None, "dp", "tensor"),
            P(None, ("tensor", "dp")),
            P(None, "tensor", "dp"),
            P(None, None, ("dp", "tensor")),
            P(None, None, ("dp", "tensor")),
            P(None, None, ("dp", "tensor")),
            P(("dp", "tensor"), None),
        ),
        check_vma=False,
    )
```

profile of v0, /device:TPU:0, one launch (start us, length us, event | category | flops | bytes accessed | tf_op | source)
XLA Modules:
  0.0 2215.0 jit_solution(16866642723154711356)
XLA Ops:
  13.8 7.2 all_gather.55
  21.9 7.1 all-gather.9.cloned.1.call-done
  43.0 16.8 reduce-scatter.45.cloned.1.call-done
  59.8 34.1 %reduce-scatter.43.cloned.1.call-done = f32[128,1024]{1,0:T(8,128)} async-done(((f32[512,1024]{1,0:T(8,128)}), f32[128,1024]{1,0:T(8,128)}) %reduce-scatter.43.cloned.1.call-update) | async-done | bytes 524304 | tf_op jit(solution)/shard_map/reduce_scatter | solution.py:98
  97.1 6.0 all_gather.57
  103.1 10.3 all-gather.11.cloned.1.call-done
  114.7 10.2 multiply_convert_fusion.3
  132.1 18.5 reduce-scatter.49.cloned.1.call-done
  150.6 34.0 %reduce-scatter.47.cloned.1.call-done = f32[128,1024]{1,0:T(8,128)} async-done(((f32[512,1024]{1,0:T(8,128)}), f32[128,1024]{1,0:T(8,128)}) %reduce-scatter.47.cloned.1.call-update) | async-done | bytes 524304 | tf_op jit(solution)/shard_map/reduce_scatter | solution.py:98
  190.0 5.8 all_gather.59
  195.8 8.4 all-gather.13.cloned.1.call-done
  219.8 18.2 reduce-scatter.53.cloned.1.call-done
  238.0 34.2 %reduce-scatter.51.cloned.1.call-done = f32[128,1024]{1,0:T(8,128)} async-done(((f32[512,1024]{1,0:T(8,128)}), f32[128,1024]{1,0:T(8,128)}) %reduce-scatter.51.cloned.1.call-update) | async-done | bytes 524304 | tf_op jit(solution)/shard_map/reduce_scatter | solution.py:98
  280.8 11.0 all-gather.15.cloned.1.call-done
  293.1 10.2 multiply_convert_fusion.2
  311.7 17.4 reduce-scatter.57.cloned.1.call-done
  329.1 34.0 %reduce-scatter.55.cloned.1.call-done = f32[128,1024]{1,0:T(8,128)} async-done(((f32[512,1024]{1,0:T(8,128)}), f32[128,1024]{1,0:T(8,128)}) %reduce-scatter.55.cloned.1.call-update) | async-done | bytes 524304 | tf_op jit(solution)/shard_map/reduce_scatter | solution.py:98
  367.5 5.8 all_gather.63
  373.2 30.6 %all_gather.62 = f32[256,128]{1,0:T(8,128)S(1)} all-gather(f32[32,128]{1,0:T(8,128)S(1)} %slice.464), channel_id=1, replica_groups=mesh['dp'=8,'tensor'=4] {'dp'}, dimensions={0}, use_global_device_ids=true | all-gather | bytes 147456 | tf_op jit(solution)/shard_map/all_gather | solution.py:403
  457.9 13.8 reduce-scatter.59.cloned.1.call-done
  473.1 63.5 %reduce-scatter.61.cloned.1.call-done = f32[32,128]{1,0:T(8,128)} async-done(((f32[256,128]{1,0:T(8,128)}), f32[32,128]{1,0:T(8,128)}) %reduce-scatter.61.cloned.1.call-update) | async-done | bytes 16400 | tf_op jit(solution)/shard_map/reduce_scatter | solution.py:419
  553.6 9.2 all-gather.17.cloned.1.call-done
  577.7 18.4 reduce-scatter.65.cloned.1.call-done
  596.1 33.8 %reduce-scatter.63.cloned.1.call-done = f32[128,1024]{1,0:T(8,128)} async-done(((f32[512,1024]{1,0:T(8,128)}), f32[128,1024]{1,0:T(8,128)}) %reduce-scatter.63.cloned.1.call-update) | async-done | bytes 524304 | tf_op jit(solution)/shard_map/reduce_scatter | solution.py:112
  636.0 5.9 all_gather.67
  642.0 8.6 all-gather.19.cloned.1.call-done
  670.8 18.4 reduce-scatter.69.cloned.1.call-done
  689.1 33.9 %reduce-scatter.67.cloned.1.call-done = f32[128,1024]{1,0:T(8,128)} async-done(((f32[512,1024]{1,0:T(8,128)}), f32[128,1024]{1,0:T(8,128)}) %reduce-scatter.67.cloned.1.call-update) | async-done | bytes 524304 | tf_op jit(solution)/shard_map/reduce_scatter | solution.py:112
  731.6 11.0 all-gather.21.cloned.1.call-done
  757.3 18.1 reduce-scatter.73.cloned.1.call-done
  775.4 34.0 %reduce-scatter.71.cloned.1.call-done = f32[128,1024]{1,0:T(8,128)} async-done(((f32[512,1024]{1,0:T(8,128)}), f32[128,1024]{1,0:T(8,128)}) %reduce-scatter.71.cloned.1.call-update) | async-done | bytes 524304 | tf_op jit(solution)/shard_map/reduce_scatter | solution.py:112
  821.3 7.5 all_gather.71
  901.2 21.6 all-reduce.2
  923.5 107.1 %reduce-scatter.105.cloned.1.call-done = f32[32,4]{1,0:T(8,128)} async-done(((f32[1024,4]{1,0:T(8,128)}), f32[32,4]{1,0:T(8,128)}) %reduce-scatter.105.cloned.1.call-update) | async-done | bytes 528
  1032.1 130.2 %reduce-scatter.103.cloned.1.call-done = f32[32,4]{1,0:T(8,128)} async-done(((f32[1024,4]{1,0:T(8,128)}), f32[32,4]{1,0:T(8,128)}) %reduce-scatter.103.cloned.1.call-update) | async-done | bytes 528
  1163.8 131.0 %reduce-scatter.101.cloned.1.call-done = f32[32,4]{1,0:T(8,128)} async-done(((f32[1024,4]{1,0:T(8,128)}), f32[32,4]{1,0:T(8,128)}) %reduce-scatter.101.cloned.1.call-update) | async-done | bytes 528
  1296.2 59.3 %reduce-scatter.97.cloned.1.call-done = f32[32,3]{1,0:T(8,128)} async-done(((f32[256,3]{1,0:T(8,128)}), f32[32,3]{1,0:T(8,128)}) %reduce-scatter.97.cloned.1.call-update) | async-done | bytes 400
  1356.9 65.4 %reduce-scatter.85.cloned.1.call-done = f32[256,128]{1,0:T(8,128)} async-done(((f32[256,1024]{1,0:T(8,128)}), f32[256,128]{1,0:T(8,128)}) %reduce-scatter.85.cloned.1.call-update) | async-done | bytes 131088 | tf_op jit(solution)/shard_map/reduce_scatter | solution.py:434
  1422.3 67.3 %reduce-scatter.83.cloned.1.call-done = f32[256,128]{1,0:T(8,128)} async-done(((f32[256,1024]{1,0:T(8,128)}), f32[256,128]{1,0:T(8,128)}) %reduce-scatter.83.cloned.1.call-update) | async-done | bytes 131088 | tf_op jit(solution)/shard_map/reduce_scatter | solution.py:434
  1491.2 89.5 %reduce-scatter.93.cloned.1.call-done = f32[1024,128]{1,0:T(8,128)} async-done(((f32[1024,1024]{1,0:T(8,128)}), f32[1024,128]{1,0:T(8,128)}) %reduce-scatter.93.cloned.1.call-update) | async-done | bytes 524304 | tf_op jit(solution)/shard_map/reduce_scatter | solution.py:437
  1580.7 92.2 %reduce-scatter.91.cloned.1.call-done = f32[1024,128]{1,0:T(8,128)} async-done(((f32[1024,1024]{1,0:T(8,128)}), f32[1024,128]{1,0:T(8,128)}) %reduce-scatter.91.cloned.1.call-update) | async-done | bytes 524304 | tf_op jit(solution)/shard_map/reduce_scatter | solution.py:437
  1675.1 89.3 %reduce-scatter.89.cloned.1.call-done = f32[128,1024]{1,0:T(8,128)} async-done(((f32[1024,1024]{1,0:T(8,128)}), f32[128,1024]{1,0:T(8,128)}) %reduce-scatter.89.cloned.1.call-update) | async-done | bytes 524304 | tf_op jit(solution)/shard_map/reduce_scatter | solution.py:435
  1764.4 91.7 %reduce-scatter.87.cloned.1.call-done = f32[128,1024]{1,0:T(8,128)} async-done(((f32[1024,1024]{1,0:T(8,128)}), f32[128,1024]{1,0:T(8,128)}) %reduce-scatter.87.cloned.1.call-update) | async-done | bytes 524304 | tf_op jit(solution)/shard_map/reduce_scatter | solution.py:435
  1858.4 22.0 reduce-scatter.77.cloned.1.call-done
  1880.5 34.0 %reduce-scatter.75.cloned.1.call-done = f32[128,1024]{1,0:T(8,128)} async-done(((f32[512,1024]{1,0:T(8,128)}), f32[128,1024]{1,0:T(8,128)}) %reduce-scatter.75.cloned.1.call-update) | async-done | bytes 524304 | tf_op jit(solution)/shard_map/reduce_scatter | solution.py:112
  1917.2 75.6 %reduce-scatter.81.cloned.1.call-done = f32[128,3,256]{2,0,1:T(8,128)} async-done(((f32[1024,3,256]{2,0,1:T(8,128)}), f32[128,3,256]{2,0,1:T(8,128)}) %reduce-scatter.81.cloned.1.call-update) | async-done | bytes 393232 | tf_op jit(solution)/shard_map/reduce_scatter | solution.py:432
  1992.8 77.6 %reduce-scatter.79.cloned.1.call-done = f32[128,3,256]{2,0,1:T(8,128)} async-done(((f32[1024,3,256]{2,0,1:T(8,128)}), f32[128,3,256]{2,0,1:T(8,128)}) %reduce-scatter.79.cloned.1.call-update) | async-done | bytes 393232 | tf_op jit(solution)/shard_map/reduce_scatter | solution.py:432
  2072.5 134.1 %reduce-scatter.95.cloned.1.call-done = f32[32,128]{1,0:T(8,128)} async-done(((f32[1024,128]{1,0:T(8,128)}), f32[32,128]{1,0:T(8,128)}) %reduce-scatter.95.cloned.1.call-update) | async-done | bytes 16400 | tf_op jit(solution)/shard_map/reduce_scatter | solution.py:453
  (667 shorter events, 309.3 us)
Async XLA Ops:
  7.2 358.1 %copy-start = (bf16[1024,128]{1,0:T(8,128)(2,1)S(1)}, bf16[1024,128]{1,0:T(8,128)(2,1)}, u32[]{:S(2)}) copy-start(bf16[1024,128]{1,0:T(8,128)(2,1)} %param.27) | copy-start | bytes 786436
  7.2 21.9 all-gather.9.cloned.1.call-start
  7.9 51.9 %reduce-scatter.45.cloned.1.call-start = ((), (), s32[]{:S(2)}) async-start(), calls=%async_computation.36 | async-start | bytes 655360 | tf_op jit(solution)/shard_map/reduce_scatter | solution.py:99
  21.6 186.0 %copy-start.15 = (f32[640,64]{0,1:T(8,128)}, f32[640,64]{0,1:T(8,128)S(1)}, u32[]{:S(2)}) copy-start(f32[640,64]{0,1:T(8,128)S(1)} %get-tuple-element.379) | copy-start | bytes 491524
  21.6 186.0 %copy-start.17 = (f32[640,64]{0,1:T(8,128)}, f32[640,64]{0,1:T(8,128)S(1)}, u32[]{:S(2)}) copy-start(f32[640,64]{0,1:T(8,128)S(1)} %get-tuple-element.380) | copy-start | bytes 491524
  38.0 56.0 %reduce-scatter.43.cloned.1.call-start = ((), (), s32[]{:S(2)}) async-start(), calls=%async_computation.35 | async-start | bytes 2621440 | tf_op jit(solution)/shard_map/reduce_scatter | solution.py:98
  39.6 73.8 %all-gather.11.cloned.1.call-start = ((), (), s32[]{:S(2)}) async-start(), calls=%async_computation.37 | async-start | bytes 1310720 | tf_op jit(solution)/shard_map/all_gather | solution.py:91
  41.6 144.7 %copy-start.75 = (f32[1,1,1024]{2,1,0:T(1,128)}, f32[1,1,1024]{2,1,0:T(1,128)S(1)}, u32[]{:S(2)}) copy-start(f32[1,1,1024]{2,1,0:T(1,128)S(1)} %get-tuple-element.382) | copy-start | bytes 12292
  96.4 54.2 %reduce-scatter.49.cloned.1.call-start = ((), (), s32[]{:S(2)}) async-start(), calls=%async_computation.39 | async-start | bytes 655360 | tf_op jit(solution)/shard_map/reduce_scatter | solution.py:99
  128.8 55.8 %reduce-scatter.47.cloned.1.call-start = ((), (), s32[]{:S(2)}) async-start(), calls=%async_computation.38 | async-start | bytes 2621440 | tf_op jit(solution)/shard_map/reduce_scatter | solution.py:98
  132.0 72.2 %all-gather.13.cloned.1.call-start = ((), (), s32[]{:S(2)}) async-start(), calls=%async_computation.40 | async-start | bytes 1310720 | tf_op jit(solution)/shard_map/all_gather | solution.py:91
  187.3 50.7 %reduce-scatter.53.cloned.1.call-start = ((), (), s32[]{:S(2)}) async-start(), calls=%async_computation.42 | async-start | bytes 655360 | tf_op jit(solution)/shard_map/reduce_scatter | solution.py:99
  216.3 55.9 %reduce-scatter.51.cloned.1.call-start = ((), (), s32[]{:S(2)}) async-start(), calls=%async_computation.41 | async-start | bytes 2621440 | tf_op jit(solution)/shard_map/reduce_scatter | solution.py:98
  219.8 72.0 %all-gather.15.cloned.1.call-start = ((), (), s32[]{:S(2)}) async-start(), calls=%async_computation.43 | async-start | bytes 1310720 | tf_op jit(solution)/shard_map/all_gather | solution.py:91
  274.9 54.2 %reduce-scatter.57.cloned.1.call-start = ((), (), s32[]{:S(2)}) async-start(), calls=%async_computation.45 | async-start | bytes 655360 | tf_op jit(solution)/shard_map/reduce_scatter | solution.py:99
  307.3 55.7 %reduce-scatter.55.cloned.1.call-start = ((), (), s32[]{:S(2)}) async-start(), calls=%async_computation.44 | async-start | bytes 2621440 | tf_op jit(solution)/shard_map/reduce_scatter | solution.py:98
  366.7 173.0 %copy-start.26 = (f32[160,128]{1,0:T(8,128)}, f32[160,128]{1,0:T(8,128)S(1)}, u32[]{:S(2)}) copy-start(f32[160,128]{1,0:T(8,128)S(1)} %get-tuple-element.417) | copy-start | bytes 245764
  419.0 11.8 all-to-all-start
  439.3 10.1 all-to-all-start.1
  443.1 28.5 %reduce-scatter.59.cloned.1.call-start = ((), (), s32[]{:S(2)}) async-start(), calls=%async_computation.46 | async-start | bytes 327680 | tf_op jit(solution)/shard_map/reduce_scatter | solution.py:418
  455.0 81.7 %reduce-scatter.61.cloned.1.call-start = ((), (), s32[]{:S(2)}) async-start(), calls=%async_computation.47 | async-start | bytes 147456 | tf_op jit(solution)/shard_map/reduce_scatter | solution.py:419
  457.9 105.0 %all-gather.17.cloned.1.call-start = ((), (), s32[]{:S(2)}) async-start(), calls=%async_computation.48 | async-start | bytes 1310720 | tf_op jit(solution)/shard_map/all_gather | solution.py:105
  546.9 49.2 %reduce-scatter.65.cloned.1.call-start = ((), (), s32[]{:S(2)}) async-start(), calls=%async_computation.50 | async-start | bytes 655360 | tf_op jit(solution)/shard_map/reduce_scatter | solution.py:113
  574.4 55.6 %reduce-scatter.63.cloned.1.call-start = ((), (), s32[]{:S(2)}) async-start(), calls=%async_computation.49 | async-start | bytes 2621440 | tf_op jit(solution)/shard_map/reduce_scatter | solution.py:112
  577.6 73.0 %all-gather.19.cloned.1.call-start = ((), (), s32[]{:S(2)}) async-start(), calls=%async_computation.51 | async-start | bytes 1310720 | tf_op jit(solution)/shard_map/all_gather | solution.py:105
  633.7 55.4 %reduce-scatter.69.cloned.1.call-start = ((), (), s32[]{:S(2)}) async-start(), calls=%async_computation.53 | async-start | bytes 655360 | tf_op jit(solution)/shard_map/reduce_scatter | solution.py:113
  667.4 55.6 %reduce-scatter.67.cloned.1.call-start = ((), (), s32[]{:S(2)}) async-start(), calls=%async_computation.52 | async-start | bytes 2621440 | tf_op jit(solution)/shard_map/reduce_scatter | solution.py:112
  670.7 72.0 %all-gather.21.cloned.1.call-start = ((), (), s32[]{:S(2)}) async-start(), calls=%async_computation.54 | async-start | bytes 1310720 | tf_op jit(solution)/shard_map/all_gather | solution.py:105
  725.8 49.6 %reduce-scatter.73.cloned.1.call-start = ((), (), s32[]{:S(2)}) async-start(), calls=%async_computation.56 | async-start | bytes 655360 | tf_op jit(solution)/shard_map/reduce_scatter | solution.py:113
  753.7 55.7 %reduce-scatter.71.cloned.1.call-start = ((), (), s32[]{:S(2)}) async-start(), calls=%async_computation.55 | async-start | bytes 2621440 | tf_op jit(solution)/shard_map/reduce_scatter | solution.py:112
  757.0 75.9 %all-gather.23.cloned.1.call-start = ((), (), s32[]{:S(2)}) async-start(), calls=%async_computation.57 | async-start | bytes 1310720 | tf_op jit(solution)/shard_map/all_gather | solution.py:105
  812.2 88.2 %reduce-scatter.99.cloned.1.call-start = ((), (), s32[]{:S(2)}) async-start(), calls=%async_computation.70 | async-start | bytes 147456
  813.1 217.5 %reduce-scatter.105.cloned.1.call-start = ((), (), s32[]{:S(2)}) async-start(), calls=%async_computation.73 | async-start | bytes 540672
  817.1 345.2 %reduce-scatter.103.cloned.1.call-start = ((), (), s32[]{:S(2)}) async-start(), calls=%async_computation.72 | async-start | bytes 540672
  821.2 473.5 %reduce-scatter.101.cloned.1.call-start = ((), (), s32[]{:S(2)}) async-start(), calls=%async_computation.71 | async-start | bytes 540672
  832.8 522.7 %reduce-scatter.97.cloned.1.call-start = ((), (), s32[]{:S(2)}) async-start(), calls=%async_computation.69 | async-start | bytes 147456
  845.2 577.1 %reduce-scatter.85.cloned.1.call-start = ((), (), s32[]{:S(2)}) async-start(), calls=%async_computation.63 | async-start | bytes 1179648 | tf_op jit(solution)/shard_map/reduce_scatter | solution.py:434
  847.8 641.7 %reduce-scatter.83.cloned.1.call-start = ((), (), s32[]{:S(2)}) async-start(), calls=%async_computation.62 | async-start | bytes 1179648 | tf_op jit(solution)/shard_map/reduce_scatter | solution.py:434
  850.9 729.9 %reduce-scatter.93.cloned.1.call-start = ((), (), s32[]{:S(2)}) async-start(), calls=%async_computation.67 | async-start | bytes 4718592 | tf_op jit(solution)/shard_map/reduce_scatter | solution.py:437
  856.1 816.8 %reduce-scatter.91.cloned.1.call-start = ((), (), s32[]{:S(2)}) async-start(), calls=%async_computation.66 | async-start | bytes 4718592 | tf_op jit(solution)/shard_map/reduce_scatter | solution.py:437
  862.6 901.8 %reduce-scatter.89.cloned.1.call-start = ((), (), s32[]{:S(2)}) async-start(), calls=%async_computation.65 | async-start | bytes 4718592 | tf_op jit(solution)/shard_map/reduce_scatter | solution.py:435
  869.1 987.0 %reduce-scatter.87.cloned.1.call-start = ((), (), s32[]{:S(2)}) async-start(), calls=%async_computation.64 | async-start | bytes 4718592 | tf_op jit(solution)/shard_map/reduce_scatter | solution.py:435
  875.5 1004.9 %reduce-scatter.77.cloned.1.call-start = ((), (), s32[]{:S(2)}) async-start(), calls=%async_computation.59 | async-start | bytes 655360 | tf_op jit(solution)/shard_map/reduce_scatter | solution.py:113
  881.7 1032.8 %reduce-scatter.75.cloned.1.call-start = ((), (), s32[]{:S(2)}) async-start(), calls=%async_computation.58 | async-start | bytes 2621440 | tf_op jit(solution)/shard_map/reduce_scatter | solution.py:112
  885.1 1107.8 %reduce-scatter.81.cloned.1.call-start = ((), (), s32[]{:S(2)}) async-start(), calls=%async_computation.61 | async-start | bytes 3538944 | tf_op jit(solution)/shard_map/reduce_scatter | solution.py:432
  889.4 1181.0 %reduce-scatter.79.cloned.1.call-start = ((), (), s32[]{:S(2)}) async-start(), calls=%async_computation.60 | async-start | bytes 3538944 | tf_op jit(solution)/shard_map/reduce_scatter | solution.py:432
  895.1 1311.5 %reduce-scatter.95.cloned.1.call-start = ((), (), s32[]{:S(2)}) async-start(), calls=%async_computation.68 | async-start | bytes 540672 | tf_op jit(solution)/shard_map/reduce_scatter | solution.py:453
  1856.1 350.5 %copy-start.1 = (bf16[1024,128]{1,0:T(8,128)(2,1)S(1)}, bf16[1024,128]{1,0:T(8,128)(2,1)}, u32[]{:S(2)}) copy-start(bf16[1024,128]{1,0:T(8,128)(2,1)} %param.27) | copy-start | bytes 786436
  (155 other events, 2718.2 us)
Sparse Core Ops, SparseCore 0:
  9.6 19.4 all-gather.8
  38.1 21.6 reduce-scatter.44
  62.5 31.3 reduce-scatter.42
  96.6 16.7 all-gather.10
  128.9 21.6 reduce-scatter.48
  153.2 31.3 reduce-scatter.46
  187.4 16.7 all-gather.12
  216.3 21.6 reduce-scatter.52
  240.7 31.4 reduce-scatter.50
  275.0 16.7 all-gather.14
  307.4 21.6 reduce-scatter.56
  331.6 31.3 reduce-scatter.54
  455.1 16.4 reduce-scatter.58
  475.8 60.8 reduce-scatter.60
  547.1 15.7 all-gather.16
  574.5 21.6 reduce-scatter.64
  598.5 31.4 reduce-scatter.62
  633.9 16.7 all-gather.18
  667.5 21.6 reduce-scatter.68
  691.5 31.4 reduce-scatter.66
  725.9 16.7 all-gather.20
  753.8 21.6 reduce-scatter.72
  777.9 31.4 reduce-scatter.70
  812.3 18.1 all-gather.22
  834.7 60.8 reduce-scatter.98
  897.8 132.7 reduce-scatter.104
  1032.7 129.5 reduce-scatter.102
  1165.2 129.5 reduce-scatter.100
  1298.7 56.7 reduce-scatter.96
  1359.3 62.9 reduce-scatter.84
  1426.7 62.8 reduce-scatter.82
  1493.2 87.4 reduce-scatter.92
  1584.6 88.2 reduce-scatter.90
  1676.5 87.8 reduce-scatter.88
  1768.4 87.6 reduce-scatter.86
  1859.0 21.3 reduce-scatter.76
  1883.0 31.4 reduce-scatter.74
  1918.1 74.7 reduce-scatter.80
  1996.3 74.1 reduce-scatter.78
  2073.3 133.2 reduce-scatter.94
where the time goes:
time: 2220 us
  waiting for transfers between devices  1780 us (80%)
  local copies, waits for them, and re-layouts  121 us (5%)
  matrix products  118 us (5%)
  blocking collectives  108 us (5%)
  other arithmetic  49.9 us (2%)
    unnamed x45, waiting for transfers between devices  429 us
    reduce_scatter x2, waiting for transfers between devices, per_device(): lax.psum_scatter(weight_grads[5], 'dp', scatter_dimension=1, tiled=True)  182 us
    reduce_scatter x2, waiting for transfers between devices, per_device(): lax.psum_scatter(weight_grads[3], 'dp', scatter_dimension=0, tiled=True)  181 us
    reduce_scatter x2, waiting for transfers between devices, per_device(): lax.psum_scatter(weight_grads[0], 'dp', scatter_dimension=0, tiled=True)  153 us
    reduce_scatter x4, waiting for transfers between devices, share_rows(): lax.psum_scatter(doc_part, 'tensor', scatter_dimension=0, tiled=True)  136 us
    reduce_scatter x4, waiting for transfers between devices, share_grads(): lax.psum_scatter(doc_part, 'tensor', scatter_dimension=0, tiled=True)  136 us
    reduce_scatter x1, waiting for transfers between devices, per_device(): lax.psum_scatter(g_w_proj, ('dp', 'tensor'), scatter_dimension=0, tiled=T...  134 us
    reduce_scatter x2, waiting for transfers between devices, per_device(): lax.psum_scatter(weight_grads[2], 'dp', scatter_dimension=1, tiled=True)  133 us
  transfers between devices with their start and end apart: 42, of which 40 were waited for; matrix products, arithmetic and copies ran while one was open for 6% of the time, Pallas kernels for 0%

commit v1 on v0

v1 whole, which is shorter than its diff:
```python
import math

import jax
import jax.numpy as jnp
from jax import lax
from jax.sharding import PartitionSpec as P

HD = 64
LAYERS = 2

precise = lax.Precision.HIGHEST
eps_norm = 1e-05
eps_unit = 1e-06
tau_token = 0.1
temp_loss = 0.1
masked_score = -1000000000.0
low = jnp.bfloat16


def inner(left, right):
    return lax.dot_general(
        left, right, (((0,), (0,)), ((), ())), preferred_element_type=jnp.float32
    )


def times_t(left, right):
    return lax.dot_general(
        left, right, (((1,), (1,)), ((), ())), preferred_element_type=jnp.float32
    )


def inner_exact(left, right):
    return lax.dot_general(
        left, right, (((0,), (0,)), ((), ())), precision=precise, preferred_element_type=jnp.float32
    )


def times_t_exact(left, right):
    return lax.dot_general(
        left, right, (((1,), (1,)), ((), ())), precision=precise, preferred_element_type=jnp.float32
    )


def layer_norm(values, gain_row, bias_row):
    average = jnp.mean(values, axis=-1, keepdims=True)
    centred = values - average
    spread = jnp.mean(centred * centred, axis=-1, keepdims=True)
    return centred * lax.rsqrt(spread + eps_norm) * gain_row + bias_row


def unit(values):
    return values * lax.rsqrt(jnp.sum(values * values, axis=-1, keepdims=True) + eps_unit)


def gelu_exact(values):
    return jax.nn.gelu(values, approximate=False)


def bits_of(axis):
    size = lax.axis_size(axis)
    assert size & (size - 1) == 0
    return [1 << k for k in reversed(range(size.bit_length() - 1))]


def relative(axis):
    order = [0]
    for bit in bits_of(axis):
        order = order + [one ^ bit for one in order]
    return order


def swap(values, axis, bit):
    return lax.ppermute(values, axis, [(i, i ^ bit) for i in range(lax.axis_size(axis))])


def gather(values, axis):
    for bit in bits_of(axis):
        values = jnp.concatenate([values, swap(values, axis, bit)], axis=0)
    return values


def scatter_sum(values, axis, kind=low):
    for bit in reversed(bits_of(axis)):
        half = values.shape[0] // 2
        taken = swap(values[half:].astype(kind), axis, bit)
        values = values[:half].astype(jnp.float32) + taken.astype(jnp.float32)
    return values


def sum_all(values, axis):
    for bit in reversed(bits_of(axis)):
        values = values + swap(values, axis, bit)
    return values


def own_part(values, index, size):
    return lax.dynamic_slice_in_dim(values, index * size, size, values.ndim - 1)


def arranged(values, own, order):
    size = values.shape[1] // len(order)
    return jnp.concatenate([own_part(values, own ^ step, size) for step in order], axis=1)


def rotary_tables(positions, head_dim):
    half_dim = head_dim // 2
    frequency = jnp.exp(jnp.arange(half_dim, dtype=jnp.float32) * (-math.log(10000.0) / half_dim))
    angles = positions.astype(jnp.float32)[:, None] * frequency[None, :]
    angles = jnp.concatenate([angles, angles], axis=1)
    return (jnp.cos(angles), jnp.sin(angles))


def rotate(values, cos_table, sine_table):
    half_dim = values.shape[-1] // 2
    turned = jnp.concatenate([-values[..., half_dim:], values[..., :half_dim]], axis=-1)
    return values * cos_table[:, None, :] + turned * sine_table[:, None, :]


def rotate_back(grads, cos_table, sine_table):
    half_dim = grads.shape[-1] // 2
    scaled = grads * sine_table[:, None, :]
    turned = jnp.concatenate([scaled[..., half_dim:], -scaled[..., :half_dim]], axis=-1)
    return grads * cos_table[:, None, :] + turned


def masked_scores(queries, keys, segment, scale_qk):
    scores = jnp.einsum("qhd,khd->hqk", queries, keys, preferred_element_type=jnp.float32) * scale_qk
    return jnp.where((segment[:, None] == segment[None, :])[None], scores, masked_score)


def attend_forward(queries, keys, values, segment):
    scores = masked_scores(queries, keys, segment, queries.shape[2] ** (-0.5))
    peak = jnp.max(scores, axis=-1, keepdims=True)
    log_total = peak + jnp.log(jnp.sum(jnp.exp(scores - peak), axis=-1, keepdims=True))
    attn_probs = jnp.exp(scores - log_total).astype(low)
    result = jnp.einsum("hqk,khd->qhd", attn_probs, values, preferred_element_type=jnp.float32)
    return (result, log_total)


def attend_backward(queries, keys, values, segment, log_total, grad_out):
    scale_qk = queries.shape[2] ** (-0.5)
    scores = masked_scores(queries, keys, segment, scale_qk)
    attn_probs = jnp.exp(scores - log_total)
    prob_grad = jnp.einsum("qhd,khd->hqk", grad_out, values, preferred_element_type=jnp.float32)
    delta_row = jnp.sum(attn_probs * prob_grad, axis=-1, keepdims=True)
    score_grad = (attn_probs * (prob_grad - delta_row)).astype(low)
    query_grad = (
        jnp.einsum("hqk,khd->qhd", score_grad, keys, preferred_element_type=jnp.float32) * scale_qk
    )
    key_grad = (
        jnp.einsum("hqk,qhd->khd", score_grad, queries, preferred_element_type=jnp.float32)
        * scale_qk
    )
    value_grad = jnp.einsum(
        "hqk,qhd->khd", attn_probs.astype(low), grad_out, preferred_element_type=jnp.float32
    )
    return (query_grad, key_grad, value_grad)


def layer_forward(state, params, layer_idx, layout):
    w_qkv, b_qkv, w_attn_out, w_ff_in, b_ff_in, w_ff_out, out_bias, norm_gain, norm_bias = params
    segment, cos_table, sine_table = layout
    inputs = gather(state.astype(low), "tensor")
    row_count, width = inputs.shape
    local_width = w_qkv.shape[3]
    mixed = jnp.dot(
        inputs, w_qkv[layer_idx].reshape(width, 3 * local_width), preferred_element_type=jnp.float32
    )
    mixed = mixed.reshape(row_count, 3, local_width) + b_qkv[layer_idx][None]
    head_shape = (row_count, local_width // HD, HD)
    queries = rotate(mixed[:, 0].reshape(head_shape), cos_table, sine_table).astype(low)
    keys = rotate(mixed[:, 1].reshape(head_shape), cos_table, sine_table).astype(low)
    values = mixed[:, 2].reshape(head_shape).astype(low)
    attended, logs = attend_forward(queries, keys, values, segment)
    attended = attended.reshape(row_count, local_width).astype(low)
    branch_terms = jnp.dot(attended, w_attn_out[layer_idx], preferred_element_type=jnp.float32)
    branch = scatter_sum(branch_terms, "tensor")
    residual = state + branch + out_bias[layer_idx, 0]
    normed = layer_norm(residual, norm_gain[layer_idx, 0], norm_bias[layer_idx, 0])
    normed_full = gather(normed.astype(low), "tensor")
    upward = (
        jnp.dot(normed_full, w_ff_in[layer_idx], preferred_element_type=jnp.float32)
        + b_ff_in[layer_idx]
    )
    activated = gelu_exact(upward).astype(low)
    ff_terms = jnp.dot(activated, w_ff_out[layer_idx], preferred_element_type=jnp.float32)
    combined = normed + scatter_sum(ff_terms, "tensor") + out_bias[layer_idx, 1]
    output = layer_norm(combined, norm_gain[layer_idx, 1], norm_bias[layer_idx, 1])
    kept = (inputs, queries, keys, values, logs, attended, residual, normed_full, upward, activated, combined)
    return (output, kept)


def layer_backward(grad_state, kept, params, layer_idx, layout, place):
    w_qkv, b_qkv, w_attn_out, w_ff_in, b_ff_in, w_ff_out, out_bias, norm_gain, norm_bias = params
    segment, cos_table, sine_table = layout
    own_dp, order = place
    (inputs, queries, keys, values, logs, attended, residual, normed_full, upward, activated, combined) = kept
    row_count, width = inputs.shape
    local_width = w_qkv.shape[3]
    _, norm_pull = jax.vjp(layer_norm, combined, norm_gain[layer_idx, 1], norm_bias[layer_idx, 1])
    g_combined, g_gain_ff, g_shift_ff = norm_pull(grad_state)
    g_branch_ff = g_combined.astype(low)
    g_bias_ff = jnp.sum(g_branch_ff, axis=0, dtype=jnp.float32)
    g_ff_full = gather(g_branch_ff, "tensor")
    g_ff_out = scatter_sum(inner(arranged(g_ff_full, own_dp, order), activated), "dp")
    g_activated = times_t(g_ff_full, w_ff_out[layer_idx])
    _, gelu_pull = jax.vjp(gelu_exact, upward)
    g_upward = gelu_pull(g_activated)[0].astype(low)
    g_b_ff_in = jnp.sum(g_upward, axis=0, dtype=jnp.float32)
    ff_back = times_t(g_upward, w_ff_in[layer_idx])
    g_ff_in = scatter_sum(inner(arranged(normed_full, own_dp, order), g_upward), "dp")
    g_normed = g_combined + scatter_sum(ff_back, "tensor")
    _, first_pull = jax.vjp(layer_norm, residual, norm_gain[layer_idx, 0], norm_bias[layer_idx, 0])
    g_residual, g_gain_attn, g_shift_attn = first_pull(g_normed)
    g_branch_attn = g_residual.astype(low)
    g_bias_attn = jnp.sum(g_branch_attn, axis=0, dtype=jnp.float32)
    g_attn_full = gather(g_branch_attn, "tensor")
    g_attn_out = scatter_sum(inner(arranged(g_attn_full, own_dp, order), attended), "dp")
    g_attended = times_t(g_attn_full, w_attn_out[layer_idx]).reshape(queries.shape).astype(low)
    gq, gk, gv = attend_backward(queries, keys, values, segment, logs, g_attended)
    g_queries = rotate_back(gq, cos_table, sine_table)
    g_keys = rotate_back(gk, cos_table, sine_table)
    g_mixed = (
        jnp.stack([g_queries, g_keys, gv], axis=1).reshape(row_count, 3 * local_width).astype(low)
    )
    g_b_qkv = jnp.sum(g_mixed, axis=0, dtype=jnp.float32)
    in_back = times_t(g_mixed, w_qkv[layer_idx].reshape(width, 3 * local_width))
    g_qkv = scatter_sum(inner(arranged(inputs, own_dp, order), g_mixed), "dp")
    g_state = g_residual + scatter_sum(in_back, "tensor")
    g_bias = sum_all(jnp.concatenate([g_b_qkv, g_b_ff_in]), "dp")
    size = local_width // len(order)
    g_b_qkv = own_part(g_bias[: 3 * local_width].reshape(3, local_width), own_dp, size)
    g_b_ff_in = own_part(g_bias[3 * local_width :], own_dp, g_b_ff_in.shape[0] // len(order))
    weight_grads = (
        g_qkv.reshape(g_qkv.shape[0], 3, local_width),
        g_b_qkv,
        g_attn_out.T,
        g_ff_in,
        g_b_ff_in,
        g_ff_out.T,
    )
    small_parts = jnp.stack([g_bias_attn, g_bias_ff, g_gain_attn, g_gain_ff, g_shift_attn, g_shift_ff])
    return (g_state, weight_grads, small_parts)


def per_device(
    doc_hidden,
    query_hidden,
    seg_lengths,
    labels,
    w_qkv,
    b_qkv,
    w_attn_out,
    w_ff_in,
    b_ff_in,
    w_ff_out,
    out_bias,
    norm_gain,
    norm_bias,
    w_proj,
):
    own_dp = lax.axis_index("dp")
    own_tensor = lax.axis_index("tensor")
    dp_size = lax.axis_size("dp")
    tensor_size = lax.axis_size("tensor")
    dp_order = relative("dp")
    tensor_order = relative("tensor")
    share_docs = doc_hidden.shape[0]
    query_len = query_hidden.shape[0]
    share = share_docs + query_len
    doc_lens = seg_lengths[0]
    doc_count = doc_lens.shape[0]
    owner = own_tensor ^ jnp.array(tensor_order, dtype=jnp.int32)
    doc_place = (owner[:, None] * share_docs + jnp.arange(share_docs, dtype=jnp.int32)[None, :])
    doc_ends = jnp.cumsum(doc_lens)
    passed = (doc_place[:, :, None] >= doc_ends[None, None, :]).astype(jnp.int32)
    doc_segment = jnp.sum(passed, axis=2)
    doc_position = doc_place - jnp.sum(passed * doc_lens[None, None, :], axis=2)
    query_segment = jnp.broadcast_to(doc_count + 1 + owner[:, None], (tensor_size, query_len))
    query_position = jnp.broadcast_to(jnp.arange(query_len, dtype=jnp.int32)[None, :], (tensor_size, query_len))
    segment = jnp.concatenate([doc_segment, query_segment], axis=1).reshape(-1)
    positions = jnp.concatenate([doc_position, query_position], axis=1).reshape(-1)
    cos_table, sine_table = rotary_tables(positions, HD)
    layout = (segment, cos_table, sine_table)
    all_labels = gather(labels, "dp")
    params = (w_qkv, b_qkv, w_attn_out, w_ff_in, b_ff_in, w_ff_out, out_bias, norm_gain, norm_bias)
    state = jnp.concatenate([doc_hidden, query_hidden], axis=0).astype(jnp.float32)
    kept_all = []
    for layer_idx in range(LAYERS):
        state, kept = layer_forward(state, params, layer_idx, layout)
        kept_all.append(kept)
    proj_exact = w_proj.astype(jnp.float32)
    projected = jnp.dot(state, proj_exact, precision=precise, preferred_element_type=jnp.float32)
    vectors = unit(projected)
    row_full = gather(vectors[:share_docs], "tensor")
    all_queries = gather(vectors[share_docs:], "dp")
    doc_seg = doc_segment.reshape(-1)
    member = (doc_seg[None, :] == jnp.arange(doc_count, dtype=jnp.int32)[:, None])
    scaled = times_t_exact(all_queries, row_full) / tau_token
    log_list = []
    for doc_pos in range(doc_count):
        masked = jnp.where(member[doc_pos][None, :], scaled, masked_score)
        peak = jnp.max(masked, axis=1)
        log_list.append(peak + jnp.log(jnp.sum(jnp.exp(masked - peak[:, None]), axis=1)))
    log_sums = jnp.stack(log_list, axis=1)
    tok_scores = tau_token * (log_sums - jnp.log(doc_lens.astype(jnp.float32))[None, :])
    query_scores = jnp.sum(tok_scores.reshape(dp_size, query_len, doc_count), axis=1)
    logits = query_scores[None]
    for level, bit in enumerate(bits_of("dp")):
        taken = swap(logits, "dp", bit).reshape(logits.shape[0], -1, 2, 1 << level, doc_count)
        taken = jnp.flip(taken, axis=2).reshape(logits.shape)
        logits = jnp.concatenate([logits, taken], axis=0)
    logits = jnp.swapaxes(logits, 0, 1) / temp_loss
    doc_index = (
        (own_dp ^ jnp.array(dp_order, dtype=jnp.int32))[:, None] * doc_count
        + jnp.arange(doc_count, dtype=jnp.int32)[None, :]
    )
    target = (doc_index[None] == all_labels[:, None, None]).astype(jnp.float32)
    peak = jnp.max(logits, axis=(1, 2), keepdims=True)
    log_total = peak + jnp.log(jnp.sum(jnp.exp(logits - peak), axis=(1, 2), keepdims=True))
    chosen = jnp.sum(target[0] * logits[0])
    query_loss = (log_total[0, 0, 0] - chosen)[None]
    g_groups = (jnp.exp(logits[:, 0] - log_total[:, 0]) - target[:, 0]) / temp_loss
    g_tok = jnp.broadcast_to(g_groups[:, None, :], (dp_size, query_len, doc_count)).reshape(
        dp_size * query_len, doc_count
    )
    member_f = member.astype(jnp.float32)
    log_spread = jnp.dot(log_sums, member_f, precision=precise, preferred_element_type=jnp.float32)
    g_spread = jnp.dot(g_tok, member_f, precision=precise, preferred_element_type=jnp.float32)
    valid = (doc_seg < doc_count)[None, :]
    g_sims = jnp.where(valid, g_spread * jnp.exp(scaled - log_spread), 0.0)
    g_all_queries = jnp.dot(g_sims, row_full, precision=precise, preferred_element_type=jnp.float32)
    g_row_docs = inner_exact(g_sims, all_queries)
    g_doc_vecs = scatter_sum(g_row_docs, "tensor", jnp.float32)
    g_query_vecs = scatter_sum(g_all_queries, "dp", jnp.float32)
    g_vectors = jnp.concatenate([g_doc_vecs, g_query_vecs], axis=0)
    _, unit_pull = jax.vjp(unit, projected)
    g_projected = unit_pull(g_vectors)[0]
    g_w_proj = inner_exact(arranged(state, own_dp, dp_order), g_projected)
    grad_state = times_t_exact(g_projected, proj_exact)
    g_w_proj = sum_all(scatter_sum(g_w_proj, "dp", jnp.float32), "tensor")
    part = g_w_proj.shape[0] // tensor_size
    g_w_proj = lax.dynamic_slice_in_dim(g_w_proj, own_tensor * part, part, 0)
    layer_grads = [None] * LAYERS
    small_list = [None] * LAYERS
    for layer_idx in reversed(range(LAYERS)):
        grad_state, weight_grads, small_parts = layer_backward(
            grad_state, kept_all[layer_idx], params, layer_idx, layout, (own_dp, dp_order)
        )
        layer_grads[layer_idx] = weight_grads
        small_list[layer_idx] = small_parts
    stacked = tuple(
        (
            jnp.stack([layer_grads[layer_pos][member_pos] for layer_pos in range(LAYERS)])
            for member_pos in range(6)
        )
    )
    small = sum_all(sum_all(jnp.stack(small_list), "tensor"), "dp")
    part = small.shape[2] // (dp_size * tensor_size)
    small = own_part(small, own_dp * tensor_size + own_tensor, part)
    return (
        query_loss,
        grad_state[:share_docs],
        grad_state[share_docs:],
        stacked[0],
        stacked[1],
        stacked[2],
        stacked[3],
        stacked[4],
        stacked[5],
        small[:, 0:2],
        small[:, 2:4],
        small[:, 4:6],
        g_w_proj,
    )


def solution(mesh):
    return jax.shard_map(
        per_device,
        mesh=mesh,
        in_specs=(
            P(("dp", "tensor"), None),
            P(("dp", "tensor"), None),
            P("dp", None),
            P(("dp", "tensor")),
            P(None, None, None, "tensor"),
            P(None, None, "tensor"),
            P(None, "tensor", None),
            P(None, None, "tensor"),
            P(None, "tensor"),
            P(None, "tensor", None),
            P(),
            P(),
            P(),
            P(),
        ),
        out_specs=(
            P(("dp", "tensor")),
            P(("dp", "tensor"), None),
            P(("dp", "tensor"), None),
            P(None, "dp", None, "tensor"),
            P(None, None, ("tensor", "dp")),
            P(None, "tensor", "dp"),
            P(None, "dp", "tensor"),
            P(None, ("tensor", "dp")),
            P(None, "tensor", "dp"),
            P(None, None, ("dp", "tensor")),
            P(None, None, ("dp", "tensor")),
            P(None, None, ("dp", "tensor")),
            P(("dp", "tensor"), None),
        ),
        check_vma=False,
    )
```

time: 2220 us -> 596 us (0.27)
  waiting for transfers between devices: 1780 us -> 223 us
  blocking collectives: 108 us -> 0 us
  starting transfers between devices: 12 us -> 90.4 us
  local copies, waits for them, and re-layouts: 121 us -> 92 us
  other arithmetic: 49.9 us -> 75.3 us
    reduce_scatter x27 -> x0, waiting for transfers between devices: 1280 us -> none  [the longest x2 182 us: per_device(): lax.psum_scatter(weight_grads[5], 'dp', scatter_dimension=1, tiled=True)]
    unnamed x45 -> x0, waiting for transfers between devices: 429 us -> none
    ppermute x0 -> x88, waiting for transfers between devices: none -> 223 us  [swap(): lax.ppermute(values, axis, [(i, i ^ bit) for i in range(lax.axis_size(axi...]
    ppermute x0 -> x88, starting transfers between devices: none -> 90.4 us  [swap(): lax.ppermute(values, axis, [(i, i ^ bit) for i in range(lax.axis_size(axi...]
    all_gather x10 -> x0, blocking collectives: 86.1 us -> none  [the longest x1 30.6 us: per_device(): all_queries = lax.all_gather(query_vecs, 'dp', axis=0, tiled=True)]
    all_gather x8 -> x0, waiting for transfers between devices: 65.8 us -> none  [the longest x4 36.8 us: gather_rows(): lax.all_gather(doc_part, 'tensor', axis=0, tiled=True)]
    unnamed x351 -> x434, local copies, waits for them, and re-layouts: 60.1 us -> 41.7 us
  transfers between devices with their start and end apart: 42 -> 88, of which waited for: 40 -> 48; matrix products, arithmetic and copies ran while one was open for 6% -> 25% of each run, Pallas kernels for 0% -> 0%
where the time goes in v1:
time: 596 us; the launch traced here: 586 us
  waiting for transfers between devices  223 us (37%)
  matrix products  98.7 us (17%)
  local copies, waits for them, and re-layouts  92 us (15%)
  starting transfers between devices  90.4 us (15%)
  other arithmetic  75.3 us (13%)
  between operations  7.09 us (1%)
    ppermute x88, waiting for transfers between devices, swap(): lax.ppermute(values, axis, [(i, i ^ bit) for i in range(lax.axis_size(axi...  223 us
    ppermute x88, starting transfers between devices, swap(): lax.ppermute(values, axis, [(i, i ^ bit) for i in range(lax.axis_size(axi...  90.4 us
    unnamed x434, local copies, waits for them, and re-layouts  41.7 us
    dot_general x2, matrix products, layer_forward(): jnp.dot(normed_full, w_ff_in[layer_idx], preferred_element_type=jnp.float32)  21.4 us
    dot_general x8, matrix products, times_t(): lax.dot_general(left, right, (((1,), (1,)), ((), ())), preferred_element_...  19.2 us
    add x34, other arithmetic, scatter_sum(): values = values[:half].astype(jnp.float32) + taken.astype(jnp.float32)  18.1 us
    dot_general x8, matrix products, inner(): lax.dot_general(left, right, (((0,), (0,)), ((), ())), preferred_element_...  14.5 us
    slice x48, local copies, waits for them, and re-layouts, scatter_sum(): taken = swap(values[half:].astype(kind), axis, bit)  13.2 us
  transfers between devices with their start and end apart: 88, of which 48 were waited for; matrix products, arithmetic and copies ran while one was open for 25% of the time, Pallas kernels for 0%

profile of v1, /device:TPU:0, one launch (start us, length us, event | category | flops | bytes accessed | tf_op | source)
XLA Modules:
  0.0 586.0 jit_solution(4828404781198360573)
XLA Ops:
  4.0 3.0 collective-permute-start
  33.9 8.6 %collective-permute-done.3 = bf16[160,1024]{1,0:T(8,128)(2,1)S(1)} collective-permute-done((bf16[160,1024]{1,0:T(8,128)(2,1)S(1)}, bf16[160,1024]{1,0:T(8,128)(2,1)S(1)}, u32[]{:S(2)}, u32[]{:S(2)}) %collective-permute-start.3) | collective-permute-done | bytes 327712 | tf_op jit(solution)/shard_map/ppermute | solution.py:73
  45.1 2.8 collective-permute-start.24
  51.6 2.4 collective-permute-done.4
  57.4 11.8 %multiply_convert_fusion.3 = (bf16[640,1024]{1,0:T(8,128)(2,1)S(1)}, f32[640,1024]{1,0:T(8,128)}, f32[640,1024]{1,0:T(8,128)}) fusion(f32[1024]{0:T(1024)S(1)} %bitcast.354, bf16[2,1024,1024]{2,1,0:T(8,128)(2,1)} %param.23, bf16[320,1024]{1,0:T(8,128)(2,1)S(1)} %collective-permute-done.5, bf16[160,1024]{1,0:T(8,128)(2,1)S(1)} %collective-permute-done.4, ...), kind=kOutput, calls=%fused_computation.35 | convolution fusion | flops 1389363200 | bytes 9965568 | tf_op jit(solution)/shard_map/dot_general | solution.py:182
  75.2 8.3 %collective-permute-done.7 = bf16[160,1024]{1,0:T(8,128)(2,1)S(1)} collective-permute-done((bf16[160,1024]{1,0:T(8,128)(2,1)S(1)}, bf16[160,1024]{1,0:T(8,128)(2,1)S(1)}, u32[]{:S(2)}, u32[]{:S(2)}) %collective-permute-start.7) | collective-permute-done | bytes 327712 | tf_op jit(solution)/shard_map/ppermute | solution.py:73
  110.4 8.0 %collective-permute-done.11 = bf16[160,1024]{1,0:T(8,128)(2,1)S(1)} collective-permute-done((bf16[160,1024]{1,0:T(8,128)(2,1)S(1)}, bf16[160,1024]{1,0:T(8,128)(2,1)S(1)}, u32[]{:S(2)}, u32[]{:S(2)}) %collective-permute-start.11) | collective-permute-done | bytes 327712 | tf_op jit(solution)/shard_map/ppermute | solution.py:73
  121.3 7.0 %collective-permute-done.12 = bf16[160,1024]{1,0:T(8,128)(2,1)S(1)} collective-permute-done((bf16[160,1024]{1,0:T(8,128)(2,1)S(1)}, bf16[160,1024]{1,0:T(8,128)(2,1)S(1)}, u32[]{:S(2)}, u32[]{:S(2)}) %collective-permute-start.12) | collective-permute-done | bytes 327712 | tf_op jit(solution)/shard_map/ppermute | solution.py:73
  130.5 9.6 %multiply_convert_fusion.2 = (bf16[640,1024]{1,0:T(8,128)(2,1)S(1)}, f32[640,1024]{1,0:T(8,128)}, f32[640,1024]{1,0:T(8,128)}) fusion(f32[1024]{0:T(1024)S(1)} %bitcast.356, bf16[2,1024,1024]{2,1,0:T(8,128)(2,1)S(1)} %copy-done.164, bf16[320,1024]{1,0:T(8,128)(2,1)S(1)} %collective-permute-done.13, bf16[160,1024]{1,0:T(8,128)(2,1)S(1)} %collective-permute-done.12, ...), kind=kOutput, calls=%fused_computation.22 | convolution fusion | flops 1389363200 | bytes 9965568 | tf_op jit(solution)/shard_map/dot_general | solution.py:182
  146.0 8.0 %collective-permute-done.15 = bf16[160,1024]{1,0:T(8,128)(2,1)S(1)} collective-permute-done((bf16[160,1024]{1,0:T(8,128)(2,1)S(1)}, bf16[160,1024]{1,0:T(8,128)(2,1)S(1)}, u32[]{:S(2)}, u32[]{:S(2)}) %collective-permute-start.15) | collective-permute-done | bytes 327712 | tf_op jit(solution)/shard_map/ppermute | solution.py:73
  157.3 2.6 collective-permute-start.16
  197.2 2.3 fusion.61
  225.0 3.1 fusion.142
  242.9 2.5 collective-permute-done.85
  247.5 3.0 convert_reduce_fusion
  261.5 4.4 collective-permute-done.35
  269.5 12.1 %collective-permute-done.75 = bf16[512,1024]{1,0:T(8,128)(2,1)S(1)} collective-permute-done((bf16[512,1024]{1,0:T(8,128)(2,1)S(1)}, bf16[512,1024]{1,0:T(8,128)(2,1)S(1)}, u32[]{:S(2)}, u32[]{:S(2)}) %collective-permute-start.75) | collective-permute-done | bytes 1048608 | tf_op jit(solution)/shard_map/ppermute | solution.py:73
  284.7 18.0 %collective-permute-done.69 = bf16[512,1024]{1,0:T(8,128)(2,1)S(1)} collective-permute-done((bf16[512,1024]{1,0:T(8,128)(2,1)S(1)}, bf16[512,1024]{1,0:T(8,128)(2,1)S(1)}, u32[]{:S(2)}, u32[]{:S(2)}) %collective-permute-start.69) | collective-permute-done | bytes 1048608 | tf_op jit(solution)/shard_map/ppermute | solution.py:73
  313.7 4.8 collective-permute-done.70
  320.8 3.7 collective-permute-start.71
  326.5 7.2 %collective-permute-done.77 = bf16[128,1024]{1,0:T(8,128)(2,1)S(1)} collective-permute-done((bf16[128,1024]{1,0:T(8,128)(2,1)}, bf16[128,1024]{1,0:T(8,128)(2,1)S(1)}, u32[]{:S(2)}, u32[]{:S(2)}) %collective-permute-start.77) | collective-permute-done | bytes 262176 | tf_op jit(solution)/shard_map/ppermute | solution.py:73
  335.6 3.4 collective-permute-done.71
  343.0 5.0 convolution_bitcast_fusion.3
  348.0 2.3 multiply_reduce_fusion.1
  359.2 3.0 fusion.182
  387.5 4.1 collective-permute-done.40
  397.4 3.0 convert_reduce_fusion.1
  405.3 2.3 fusion.188
  409.9 4.7 collective-permute-done.43
  416.3 3.5 fusion.186
  424.0 2.3 collective-permute-start.53
  427.6 8.3 %collective-permute-done.53 = bf16[128,768]{0,1:T(8,128)(2,1)S(1)} collective-permute-done((bf16[128,768]{0,1:T(8,128)(2,1)S(1)}, bf16[128,768]{0,1:T(8,128)(2,1)S(1)}, u32[]{:S(2)}, u32[]{:S(2)}) %collective-permute-start.53) | collective-permute-done | bytes 196640 | tf_op jit(solution)/shard_map/ppermute | solution.py:73
  438.2 20.0 %collective-permute-done.80 = f32[2,6,1024]{2,1,0:T(8,128)S(1)} collective-permute-done((f32[2,6,1024]{2,1,0:T(8,128)S(1)}, f32[2,6,1024]{2,1,0:T(8,128)S(1)}, u32[]{:S(2)}, u32[]{:S(2)}) %collective-permute-start.80) | collective-permute-done | bytes 49184 | tf_op jit(solution)/shard_map/ppermute | solution.py:73
  459.1 2.6 slice_add_fusion.1
  462.6 2.7 collective-permute-start.82
  468.0 8.4 %collective-permute-done.82 = f32[2,6,1024]{2,1,0:T(8,128)S(1)} collective-permute-done((f32[2,6,1024]{2,1,0:T(8,128)S(1)}, f32[2,6,1024]{2,1,0:T(8,128)S(1)}, u32[]{:S(2)}, u32[]{:S(2)}) %collective-permute-start.82) | collective-permute-done | bytes 49184 | tf_op jit(solution)/shard_map/ppermute | solution.py:73
  478.2 3.4 collective-permute-start.74
  481.6 10.9 %collective-permute-done.67 = bf16[256,1024]{1,0:T(8,128)(2,1)S(1)} collective-permute-done((bf16[256,1024]{1,0:T(8,128)(2,1)S(1)}, bf16[256,1024]{1,0:T(8,128)(2,1)S(1)}, u32[]{:S(2)}, u32[]{:S(2)}) %collective-permute-start.67) | collective-permute-done | bytes 524320 | tf_op jit(solution)/shard_map/ppermute | solution.py:73
  495.2 10.9 %collective-permute-done.68 = bf16[128,1024]{1,0:T(8,128)(2,1)} collective-permute-done((bf16[128,1024]{1,0:T(8,128)(2,1)}, bf16[128,1024]{1,0:T(8,128)(2,1)}, u32[]{:S(2)}, u32[]{:S(2)}) %collective-permute-start.68) | collective-permute-done | bytes 262176 | tf_op jit(solution)/shard_map/ppermute | solution.py:73
  510.6 4.8 convolution_bitcast_fusion
  515.5 2.3 multiply_reduce_fusion
  529.8 2.7 fusion.183
  534.2 3.0 collective-permute-start.56
  542.5 4.3 collective-permute-done.61
  547.7 4.6 collective-permute-done.62
  552.3 7.5 %collective-permute-done.48 = bf16[512,768]{0,1:T(8,128)(2,1)} collective-permute-done((bf16[512,768]{0,1:T(8,128)(2,1)S(1)}, bf16[512,768]{0,1:T(8,128)(2,1)}, u32[]{:S(2)}, u32[]{:S(2)}) %collective-permute-start.48) | collective-permute-done | bytes 786464 | tf_op jit(solution)/shard_map/ppermute | solution.py:73
  567.6 5.0 collective-permute-done.49
  577.0 6.5 %collective-permute-done.50 = bf16[128,768]{0,1:T(8,128)(2,1)S(1)} collective-permute-done((bf16[128,768]{0,1:T(8,128)(2,1)S(1)}, bf16[128,768]{0,1:T(8,128)(2,1)S(1)}, u32[]{:S(2)}, u32[]{:S(2)}) %collective-permute-start.50) | collective-permute-done | bytes 196640 | tf_op jit(solution)/shard_map/ppermute | solution.py:73
  (895 shorter events, 304.3 us)
Async XLA Ops:
  4.0 12.6 %collective-permute-start = (bf16[160,1024]{1,0:T(8,128)(2,1)}, bf16[160,1024]{1,0:T(8,128)(2,1)}, u32[]{:S(2)}, u32[]{:S(2)}) collective-permute-start(bf16[160,1024]{1,0:T(8,128)(2,1)} %get-tuple-element.157), channel_id=1, source_target_pairs={{0,2},{1,3},{2,0},{3,1},{4,6},{5,7},{6,4},{7,5},{8,10},{9,11},{10,... | collective-permute-start | bytes 983048 | tf_op jit(solution)/shard_map/ppermute | solution.py:73
  32.5 10.1 %collective-permute-start.3 = (bf16[160,1024]{1,0:T(8,128)(2,1)S(1)}, bf16[160,1024]{1,0:T(8,128)(2,1)S(1)}, u32[]{:S(2)}, u32[]{:S(2)}) collective-permute-start(bf16[160,1024]{1,0:T(8,128)(2,1)S(1)} %slice.1086), channel_id=1, source_target_pairs={{0,2},{1,3},{2,0},{3,1},{4,6},{5,7},{6,4},{7,5},{8,10},{9,11},{10,... | collective-permute-start | bytes 983048 | tf_op jit(solution)/shard_map/ppermute | solution.py:73
  44.8 9.2 %collective-permute-start.4 = (bf16[160,1024]{1,0:T(8,128)(2,1)S(1)}, bf16[160,1024]{1,0:T(8,128)(2,1)S(1)}, u32[]{:S(2)}, u32[]{:S(2)}) collective-permute-start(bf16[160,1024]{1,0:T(8,128)(2,1)S(1)} %fusion.92), channel_id=1, source_target_pairs={{0,2},{1,3},{2,0},{3,1},{4,6},{5,7},{6,4},{7,5},{8,10},{9,11},{10,... | collective-permute-start | bytes 983048 | tf_op jit(solution)/shard_map/ppermute | solution.py:73
  45.1 39.9 %collective-permute-start.24 = (s32[1]{0:T(128)}, s32[1]{0:T(128)}, u32[]{:S(2)}, u32[]{:S(2)}) collective-permute-start(s32[1]{0:T(128)} %param.19), channel_id=1, source_target_pairs={{0,16},{4,20},{8,24},{12,28},{16,0},{20,4},{24,8},{28,12},{1,17},{... | collective-permute-start | bytes 20 | tf_op jit(solution)/shard_map/ppermute | solution.py:73
  73.5 10.1 %collective-permute-start.7 = (bf16[160,1024]{1,0:T(8,128)(2,1)S(1)}, bf16[160,1024]{1,0:T(8,128)(2,1)S(1)}, u32[]{:S(2)}, u32[]{:S(2)}) collective-permute-start(bf16[160,1024]{1,0:T(8,128)(2,1)S(1)} %slice.1085), channel_id=1, source_target_pairs={{0,2},{1,3},{2,0},{3,1},{4,6},{5,7},{6,4},{7,5},{8,10},{9,11},{10,... | collective-permute-start | bytes 983048 | tf_op jit(solution)/shard_map/ppermute | solution.py:73
  84.4 9.8 %collective-permute-start.8 = (bf16[160,1024]{1,0:T(8,128)(2,1)S(1)}, bf16[160,1024]{1,0:T(8,128)(2,1)S(1)}, u32[]{:S(2)}, u32[]{:S(2)}) collective-permute-start(bf16[160,1024]{1,0:T(8,128)(2,1)S(1)} %fusion.93), channel_id=1, source_target_pairs={{0,2},{1,3},{2,0},{3,1},{4,6},{5,7},{6,4},{7,5},{8,10},{9,11},{10,... | collective-permute-start | bytes 983048 | tf_op jit(solution)/shard_map/ppermute | solution.py:73
  108.6 9.8 %collective-permute-start.11 = (bf16[160,1024]{1,0:T(8,128)(2,1)S(1)}, bf16[160,1024]{1,0:T(8,128)(2,1)S(1)}, u32[]{:S(2)}, u32[]{:S(2)}) collective-permute-start(bf16[160,1024]{1,0:T(8,128)(2,1)S(1)} %slice.1083), channel_id=1, source_target_pairs={{0,2},{1,3},{2,0},{3,1},{4,6},{5,7},{6,4},{7,5},{8,10},{9,11},{10,... | collective-permute-start | bytes 983048 | tf_op jit(solution)/shard_map/ppermute | solution.py:73
  119.3 9.0 %collective-permute-start.12 = (bf16[160,1024]{1,0:T(8,128)(2,1)S(1)}, bf16[160,1024]{1,0:T(8,128)(2,1)S(1)}, u32[]{:S(2)}, u32[]{:S(2)}) collective-permute-start(bf16[160,1024]{1,0:T(8,128)(2,1)S(1)} %fusion.94), channel_id=1, source_target_pairs={{0,2},{1,3},{2,0},{3,1},{4,6},{5,7},{6,4},{7,5},{8,10},{9,11},{10,... | collective-permute-start | bytes 983048 | tf_op jit(solution)/shard_map/ppermute | solution.py:73
  144.2 9.8 %collective-permute-start.15 = (bf16[160,1024]{1,0:T(8,128)(2,1)S(1)}, bf16[160,1024]{1,0:T(8,128)(2,1)S(1)}, u32[]{:S(2)}, u32[]{:S(2)}) collective-permute-start(bf16[160,1024]{1,0:T(8,128)(2,1)S(1)} %slice.1082), channel_id=1, source_target_pairs={{0,2},{1,3},{2,0},{3,1},{4,6},{5,7},{6,4},{7,5},{8,10},{9,11},{10,... | collective-permute-start | bytes 983048 | tf_op jit(solution)/shard_map/ppermute | solution.py:73
  230.4 7.3 %collective-permute-start.32 = (bf16[160,1024]{1,0:T(8,128)(2,1)S(1)}, bf16[160,1024]{1,0:T(8,128)(2,1)S(1)}, u32[]{:S(2)}, u32[]{:S(2)}) collective-permute-start(bf16[160,1024]{1,0:T(8,128)(2,1)S(1)} %get-tuple-element.83), channel_id=1, source_target_pairs={{0,2},{1,3},{2,0},{3,1},{4,6},{5,7},{6,4},{7,5},{8,10},{9,11},{10,... | collective-permute-start | bytes 983048 | tf_op jit(solution)/shard_map/ppermute | solution.py:73
  237.7 7.7 %collective-permute-start.33 = (bf16[320,1024]{1,0:T(8,128)(2,1)S(1)}, bf16[320,1024]{1,0:T(8,128)(2,1)S(1)}, u32[]{:S(2)}, u32[]{:S(2)}) collective-permute-start(bf16[320,1024]{1,0:T(8,128)(2,1)S(1)} %pad_maximum_fusion.14), channel_id=1, source_target_pairs={{0,1},{1,0},{2,3},{3,2},{4,5},{5,4},{6,7},{7,6},{8,9},{9,8},{10,11... | collective-permute-start | bytes 1966088 | tf_op jit(solution)/shard_map/ppermute | solution.py:73
  245.4 62.1 %collective-permute-start.86 = (f32[128,128]{1,0:T(8,128)S(1)}, f32[128,128]{1,0:T(8,128)S(1)}, u32[]{:S(2)}, u32[]{:S(2)}) collective-permute-start(f32[128,128]{1,0:T(8,128)S(1)} %slice_add_fusion.43), channel_id=1, source_target_pairs={{0,1},{1,0},{2,3},{3,2},{4,5},{5,4},{6,7},{7,6},{8,9},{9,8},{10,11... | collective-permute-start | bytes 196616 | tf_op jit(solution)/shard_map/ppermute | solution.py:73
  255.5 26.1 %collective-permute-start.75 = (bf16[512,1024]{1,0:T(8,128)(2,1)S(1)}, bf16[512,1024]{1,0:T(8,128)(2,1)S(1)}, u32[]{:S(2)}, u32[]{:S(2)}) collective-permute-start(bf16[512,1024]{1,0:T(8,128)(2,1)S(1)} %slice.1058), channel_id=1, source_target_pairs={{0,4},{4,0},{8,12},{12,8},{16,20},{20,16},{24,28},{28,24},{1,5},{5... | collective-permute-start | bytes 3145736 | tf_op jit(solution)/shard_map/ppermute | solution.py:73
  256.8 9.0 %collective-permute-start.35 = (bf16[160,1024]{1,0:T(8,128)(2,1)S(1)}, bf16[160,1024]{1,0:T(8,128)(2,1)S(1)}, u32[]{:S(2)}, u32[]{:S(2)}) collective-permute-start(bf16[160,1024]{1,0:T(8,128)(2,1)S(1)} %slice.1081), channel_id=1, source_target_pairs={{0,2},{1,3},{2,0},{3,1},{4,6},{5,7},{6,4},{7,5},{8,10},{9,11},{10,... | collective-permute-start | bytes 983048 | tf_op jit(solution)/shard_map/ppermute | solution.py:73
  260.5 42.2 %collective-permute-start.69 = (bf16[512,1024]{1,0:T(8,128)(2,1)S(1)}, bf16[512,1024]{1,0:T(8,128)(2,1)S(1)}, u32[]{:S(2)}, u32[]{:S(2)}) collective-permute-start(bf16[512,1024]{1,0:T(8,128)(2,1)S(1)} %slice.1060), channel_id=1, source_target_pairs={{0,4},{4,0},{8,12},{12,8},{16,20},{20,16},{24,28},{28,24},{1,5},{5... | collective-permute-start | bytes 3145736 | tf_op jit(solution)/shard_map/ppermute | solution.py:73
  267.9 41.2 %collective-permute-start.36 = (bf16[160,1024]{1,0:T(8,128)(2,1)S(1)}, bf16[160,1024]{1,0:T(8,128)(2,1)S(1)}, u32[]{:S(2)}, u32[]{:S(2)}) collective-permute-start(bf16[160,1024]{1,0:T(8,128)(2,1)S(1)} %get-tuple-element.85), channel_id=1, source_target_pairs={{0,2},{1,3},{2,0},{3,1},{4,6},{5,7},{6,4},{7,5},{8,10},{9,11},{10,... | collective-permute-start | bytes 983048 | tf_op jit(solution)/shard_map/ppermute | solution.py:73
  283.1 26.9 %collective-permute-start.76 = (bf16[256,1024]{1,0:T(8,128)(2,1)}, bf16[256,1024]{1,0:T(8,128)(2,1)}, u32[]{:S(2)}, u32[]{:S(2)}) collective-permute-start(bf16[256,1024]{1,0:T(8,128)(2,1)} %slice.1072), channel_id=1, source_target_pairs={{0,8},{4,12},{8,0},{12,4},{16,24},{20,28},{24,16},{28,20},{1,9},{5... | collective-permute-start | bytes 1572872 | tf_op jit(solution)/shard_map/ppermute | solution.py:73
  304.5 14.0 %collective-permute-start.70 = (bf16[256,1024]{1,0:T(8,128)(2,1)}, bf16[256,1024]{1,0:T(8,128)(2,1)}, u32[]{:S(2)}, u32[]{:S(2)}) collective-permute-start(bf16[256,1024]{1,0:T(8,128)(2,1)} %slice.1074), channel_id=1, source_target_pairs={{0,8},{4,12},{8,0},{12,4},{16,24},{20,28},{24,16},{28,20},{1,9},{5... | collective-permute-start | bytes 1572872 | tf_op jit(solution)/shard_map/ppermute | solution.py:73
  307.5 17.0 %collective-permute-start.87 = (f32[128,128]{1,0:T(8,128)S(1)}, f32[128,128]{1,0:T(8,128)S(1)}, u32[]{:S(2)}, u32[]{:S(2)}) collective-permute-start(f32[128,128]{1,0:T(8,128)S(1)} %add.812), channel_id=1, source_target_pairs={{0,2},{1,3},{2,0},{3,1},{4,6},{5,7},{6,4},{7,5},{8,10},{9,11},{10,... | collective-permute-start | bytes 196616 | tf_op jit(solution)/shard_map/ppermute | solution.py:73
  310.0 30.9 %collective-permute-start.37 = (bf16[320,1024]{1,0:T(8,128)(2,1)}, bf16[320,1024]{1,0:T(8,128)(2,1)}, u32[]{:S(2)}, u32[]{:S(2)}) collective-permute-start(bf16[320,1024]{1,0:T(8,128)(2,1)} %pad_maximum_fusion.15), channel_id=1, source_target_pairs={{0,1},{1,0},{2,3},{3,2},{4,5},{5,4},{6,7},{7,6},{8,9},{9,8},{10,11... | collective-permute-start | bytes 1966088 | tf_op jit(solution)/shard_map/ppermute | solution.py:73
  312.3 21.4 %collective-permute-start.77 = (bf16[128,1024]{1,0:T(8,128)(2,1)}, bf16[128,1024]{1,0:T(8,128)(2,1)S(1)}, u32[]{:S(2)}, u32[]{:S(2)}) collective-permute-start(bf16[128,1024]{1,0:T(8,128)(2,1)} %slice.1088), channel_id=1, source_target_pairs={{0,16},{4,20},{8,24},{12,28},{16,0},{20,4},{24,8},{28,12},{1,17},{... | collective-permute-start | bytes 786440 | tf_op jit(solution)/shard_map/ppermute | solution.py:73
  320.8 18.2 %collective-permute-start.71 = (bf16[128,1024]{1,0:T(8,128)(2,1)}, bf16[128,1024]{1,0:T(8,128)(2,1)S(1)}, u32[]{:S(2)}, u32[]{:S(2)}) collective-permute-start(bf16[128,1024]{1,0:T(8,128)(2,1)} %slice.1090), channel_id=1, source_target_pairs={{0,16},{4,20},{8,24},{12,28},{16,0},{20,4},{24,8},{28,12},{1,17},{... | collective-permute-start | bytes 786440 | tf_op jit(solution)/shard_map/ppermute | solution.py:73
  362.4 7.5 %collective-permute-start.38 = (bf16[320,1024]{1,0:T(8,128)(2,1)S(1)}, bf16[320,1024]{1,0:T(8,128)(2,1)S(1)}, u32[]{:S(2)}, u32[]{:S(2)}) collective-permute-start(bf16[320,1024]{1,0:T(8,128)(2,1)S(1)} %slice.1066), channel_id=1, source_target_pairs={{0,1},{1,0},{2,3},{3,2},{4,5},{5,4},{6,7},{7,6},{8,9},{9,8},{10,11... | collective-permute-start | bytes 1966088 | tf_op jit(solution)/shard_map/ppermute | solution.py:73
  366.9 11.1 %collective-permute-start.63 = (bf16[512,256]{1,0:T(8,128)(2,1)S(1)}, bf16[512,256]{1,0:T(8,128)(2,1)S(1)}, u32[]{:S(2)}, u32[]{:S(2)}) collective-permute-start(bf16[512,256]{1,0:T(8,128)(2,1)S(1)} %slice.1092), channel_id=1, source_target_pairs={{0,4},{4,0},{8,12},{12,8},{16,20},{20,16},{24,28},{28,24},{1,5},{5... | collective-permute-start | bytes 786440 | tf_op jit(solution)/shard_map/ppermute | solution.py:73
  370.1 11.0 %collective-permute-start.39 = (bf16[160,1024]{1,0:T(8,128)(2,1)S(1)}, bf16[160,1024]{1,0:T(8,128)(2,1)S(1)}, u32[]{:S(2)}, u32[]{:S(2)}) collective-permute-start(bf16[160,1024]{1,0:T(8,128)(2,1)S(1)} %slice.1080), channel_id=1, source_target_pairs={{0,2},{1,3},{2,0},{3,1},{4,6},{5,7},{6,4},{7,5},{8,10},{9,11},{10,... | collective-permute-start | bytes 983048 | tf_op jit(solution)/shard_map/ppermute | solution.py:73
  374.5 19.2 %collective-permute-start.51 = (bf16[512,768]{0,1:T(8,128)(2,1)}, bf16[512,768]{0,1:T(8,128)(2,1)}, u32[]{:S(2)}, u32[]{:S(2)}) collective-permute-start(bf16[512,768]{0,1:T(8,128)(2,1)} %slice.1062), channel_id=1, source_target_pairs={{0,4},{4,0},{8,12},{12,8},{16,20},{20,16},{24,28},{28,24},{1,5},{5... | collective-permute-start | bytes 2359304 | tf_op jit(solution)/shard_map/ppermute | solution.py:73
  384.5 7.1 %collective-permute-start.40 = (bf16[160,1024]{1,0:T(8,128)(2,1)S(1)}, bf16[160,1024]{1,0:T(8,128)(2,1)S(1)}, u32[]{:S(2)}, u32[]{:S(2)}) collective-permute-start(bf16[160,1024]{1,0:T(8,128)(2,1)S(1)} %get-tuple-element.79), channel_id=1, source_target_pairs={{0,2},{1,3},{2,0},{3,1},{4,6},{5,7},{6,4},{7,5},{8,10},{9,11},{10,... | collective-permute-start | bytes 983048 | tf_op jit(solution)/shard_map/ppermute | solution.py:73
  385.9 7.2 %collective-permute-start.65 = (bf16[128,256]{1,0:T(8,128)(2,1)S(1)}, bf16[128,256]{1,0:T(8,128)(2,1)S(1)}, u32[]{:S(2)}, u32[]{:S(2)}) collective-permute-start(bf16[128,256]{1,0:T(8,128)(2,1)S(1)} %slice.1098), channel_id=1, source_target_pairs={{0,16},{4,20},{8,24},{12,28},{16,0},{20,4},{24,8},{28,12},{1,17},{... | collective-permute-start | bytes 196616 | tf_op jit(solution)/shard_map/ppermute | solution.py:73
  396.1 26.7 %collective-permute-start.52 = (bf16[256,768]{0,1:T(8,128)(2,1)}, bf16[256,768]{0,1:T(8,128)(2,1)}, u32[]{:S(2)}, u32[]{:S(2)}) collective-permute-start(bf16[256,768]{0,1:T(8,128)(2,1)} %slice.1076), channel_id=1, source_target_pairs={{0,8},{4,12},{8,0},{12,4},{16,24},{20,28},{24,16},{28,20},{1,9},{5... | collective-permute-start | bytes 1179656 | tf_op jit(solution)/shard_map/ppermute | solution.py:73
  404.6 10.1 %collective-permute-start.43 = (bf16[160,1024]{1,0:T(8,128)(2,1)S(1)}, bf16[160,1024]{1,0:T(8,128)(2,1)S(1)}, u32[]{:S(2)}, u32[]{:S(2)}) collective-permute-start(bf16[160,1024]{1,0:T(8,128)(2,1)S(1)} %slice.1079), channel_id=1, source_target_pairs={{0,2},{1,3},{2,0},{3,1},{4,6},{5,7},{6,4},{7,5},{8,10},{9,11},{10,... | collective-permute-start | bytes 983048 | tf_op jit(solution)/shard_map/ppermute | solution.py:73
  409.0 50.1 %collective-permute-start.72 = (bf16[512,1024]{1,0:T(8,128)(2,1)}, bf16[512,1024]{1,0:T(8,128)(2,1)}, u32[]{:S(2)}, u32[]{:S(2)}) collective-permute-start(bf16[512,1024]{1,0:T(8,128)(2,1)} %slice.1059), channel_id=1, source_target_pairs={{0,4},{4,0},{8,12},{12,8},{16,20},{20,16},{24,28},{28,24},{1,5},{5... | collective-permute-start | bytes 3145736 | tf_op jit(solution)/shard_map/ppermute | solution.py:73
  421.1 44.2 %collective-permute-start.66 = (bf16[512,1024]{1,0:T(8,128)(2,1)}, bf16[512,1024]{1,0:T(8,128)(2,1)}, u32[]{:S(2)}, u32[]{:S(2)}) collective-permute-start(bf16[512,1024]{1,0:T(8,128)(2,1)} %slice.1061), channel_id=1, source_target_pairs={{0,4},{4,0},{8,12},{12,8},{16,20},{20,16},{24,28},{28,24},{1,5},{5... | collective-permute-start | bytes 3145736 | tf_op jit(solution)/shard_map/ppermute | solution.py:73
  424.0 11.9 %collective-permute-start.53 = (bf16[128,768]{0,1:T(8,128)(2,1)S(1)}, bf16[128,768]{0,1:T(8,128)(2,1)S(1)}, u32[]{:S(2)}, u32[]{:S(2)}) collective-permute-start(bf16[128,768]{0,1:T(8,128)(2,1)S(1)} %slice.1094), channel_id=1, source_target_pairs={{0,16},{4,20},{8,24},{12,28},{16,0},{20,4},{24,8},{28,12},{1,17},{... | collective-permute-start | bytes 589832 | tf_op jit(solution)/shard_map/ppermute | solution.py:73
  426.5 31.8 %collective-permute-start.80 = (f32[2,6,1024]{2,1,0:T(8,128)S(1)}, f32[2,6,1024]{2,1,0:T(8,128)S(1)}, u32[]{:S(2)}, u32[]{:S(2)}) collective-permute-start(f32[2,6,1024]{2,1,0:T(8,128)S(1)} %fusion.247), channel_id=1, source_target_pairs={{0,4},{4,0},{8,12},{12,8},{16,20},{20,16},{24,28},{28,24},{1,5},{5... | collective-permute-start | bytes 147464 | tf_op jit(solution)/shard_map/ppermute | solution.py:73
  436.9 40.2 %collective-permute-start.44 = (bf16[160,1024]{1,0:T(8,128)(2,1)S(1)}, bf16[160,1024]{1,0:T(8,128)(2,1)S(1)}, u32[]{:S(2)}, u32[]{:S(2)}) collective-permute-start(bf16[160,1024]{1,0:T(8,128)(2,1)S(1)} %get-tuple-element.81), channel_id=1, source_target_pairs={{0,2},{1,3},{2,0},{3,1},{4,6},{5,7},{6,4},{7,5},{8,10},{9,11},{10,... | collective-permute-start | bytes 983048 | tf_op jit(solution)/shard_map/ppermute | solution.py:73
  461.7 16.3 %collective-permute-start.73 = (bf16[256,1024]{1,0:T(8,128)(2,1)S(1)}, bf16[256,1024]{1,0:T(8,128)(2,1)S(1)}, u32[]{:S(2)}, u32[]{:S(2)}) collective-permute-start(bf16[256,1024]{1,0:T(8,128)(2,1)S(1)} %slice.1073), channel_id=1, source_target_pairs={{0,8},{4,12},{8,0},{12,4},{16,24},{20,28},{24,16},{28,20},{1,9},{5... | collective-permute-start | bytes 1572872 | tf_op jit(solution)/shard_map/ppermute | solution.py:73
  462.6 13.8 %collective-permute-start.82 = (f32[2,6,1024]{2,1,0:T(8,128)S(1)}, f32[2,6,1024]{2,1,0:T(8,128)S(1)}, u32[]{:S(2)}, u32[]{:S(2)}) collective-permute-start(f32[2,6,1024]{2,1,0:T(8,128)S(1)} %add.805), channel_id=1, source_target_pairs={{0,16},{4,20},{8,24},{12,28},{16,0},{20,4},{24,8},{28,12},{1,17},{... | collective-permute-start | bytes 147464 | tf_op jit(solution)/shard_map/ppermute | solution.py:73
  467.1 25.4 %collective-permute-start.67 = (bf16[256,1024]{1,0:T(8,128)(2,1)S(1)}, bf16[256,1024]{1,0:T(8,128)(2,1)S(1)}, u32[]{:S(2)}, u32[]{:S(2)}) collective-permute-start(bf16[256,1024]{1,0:T(8,128)(2,1)S(1)} %slice.1075), channel_id=1, source_target_pairs={{0,8},{4,12},{8,0},{12,4},{16,24},{20,28},{24,16},{28,20},{1,9},{5... | collective-permute-start | bytes 1572872 | tf_op jit(solution)/shard_map/ppermute | solution.py:73
  478.0 30.3 %collective-permute-start.45 = (bf16[320,1024]{1,0:T(8,128)(2,1)}, bf16[320,1024]{1,0:T(8,128)(2,1)}, u32[]{:S(2)}, u32[]{:S(2)}) collective-permute-start(bf16[320,1024]{1,0:T(8,128)(2,1)} %pad_maximum_fusion.17), channel_id=1, source_target_pairs={{0,1},{1,0},{2,3},{3,2},{4,5},{5,4},{6,7},{7,6},{8,9},{9,8},{10,11... | collective-permute-start | bytes 1966088 | tf_op jit(solution)/shard_map/ppermute | solution.py:73
  478.2 15.4 %collective-permute-start.74 = (bf16[128,1024]{1,0:T(8,128)(2,1)S(1)}, bf16[128,1024]{1,0:T(8,128)(2,1)S(1)}, u32[]{:S(2)}, u32[]{:S(2)}) collective-permute-start(bf16[128,1024]{1,0:T(8,128)(2,1)S(1)} %slice.1089), channel_id=1, source_target_pairs={{0,16},{4,20},{8,24},{12,28},{16,0},{20,4},{24,8},{28,12},{1,17},{... | collective-permute-start | bytes 786440 | tf_op jit(solution)/shard_map/ppermute | solution.py:73
  493.5 12.5 %collective-permute-start.68 = (bf16[128,1024]{1,0:T(8,128)(2,1)}, bf16[128,1024]{1,0:T(8,128)(2,1)}, u32[]{:S(2)}, u32[]{:S(2)}) collective-permute-start(bf16[128,1024]{1,0:T(8,128)(2,1)} %slice.1091), channel_id=1, source_target_pairs={{0,16},{4,20},{8,24},{12,28},{16,0},{20,4},{24,8},{28,12},{1,17},{... | collective-permute-start | bytes 786440 | tf_op jit(solution)/shard_map/ppermute | solution.py:73
  528.6 13.0 %collective-permute-start.60 = (bf16[512,256]{1,0:T(8,128)(2,1)S(1)}, bf16[512,256]{1,0:T(8,128)(2,1)S(1)}, u32[]{:S(2)}, u32[]{:S(2)}) collective-permute-start(bf16[512,256]{1,0:T(8,128)(2,1)S(1)} %slice.1093), channel_id=1, source_target_pairs={{0,4},{4,0},{8,12},{12,8},{16,20},{20,16},{24,28},{28,24},{1,5},{5... | collective-permute-start | bytes 786440 | tf_op jit(solution)/shard_map/ppermute | solution.py:73
  533.6 28.8 %collective-permute-start.46 = (bf16[320,1024]{1,0:T(8,128)(2,1)}, bf16[320,1024]{1,0:T(8,128)(2,1)}, u32[]{:S(2)}, u32[]{:S(2)}) collective-permute-start(bf16[320,1024]{1,0:T(8,128)(2,1)} %slice.1064), channel_id=1, source_target_pairs={{0,1},{1,0},{2,3},{3,2},{4,5},{5,4},{6,7},{7,6},{8,9},{9,8},{10,11... | collective-permute-start | bytes 1966088 | tf_op jit(solution)/shard_map/ppermute | solution.py:73
  534.2 7.3 %collective-permute-start.56 = (f32[1792]{0:T(1024)S(1)}, f32[1792]{0:T(1024)S(1)}, u32[]{:S(2)}, u32[]{:S(2)}) collective-permute-start(f32[1792]{0:T(1024)S(1)} %add.778), channel_id=1, source_target_pairs={{0,16},{4,20},{8,24},{12,28},{16,0},{20,4},{24,8},{28,12},{1,17},{... | collective-permute-start | bytes 21512 | tf_op jit(solution)/shard_map/ppermute | solution.py:73
  540.5 19.3 %collective-permute-start.48 = (bf16[512,768]{0,1:T(8,128)(2,1)S(1)}, bf16[512,768]{0,1:T(8,128)(2,1)}, u32[]{:S(2)}, u32[]{:S(2)}) collective-permute-start(bf16[512,768]{0,1:T(8,128)(2,1)S(1)} %slice.1063), channel_id=1, source_target_pairs={{0,4},{4,0},{8,12},{12,8},{16,20},{20,16},{24,28},{28,24},{1,5},{5... | collective-permute-start | bytes 2359304 | tf_op jit(solution)/shard_map/ppermute | solution.py:73
  562.4 10.1 %collective-permute-start.49 = (bf16[256,768]{0,1:T(8,128)(2,1)}, bf16[256,768]{0,1:T(8,128)(2,1)}, u32[]{:S(2)}, u32[]{:S(2)}) collective-permute-start(bf16[256,768]{0,1:T(8,128)(2,1)} %slice.1077), channel_id=1, source_target_pairs={{0,8},{4,12},{8,0},{12,4},{16,24},{20,28},{24,16},{28,20},{1,9},{5... | collective-permute-start | bytes 1179656 | tf_op jit(solution)/shard_map/ppermute | solution.py:73
  564.5 9.9 %collective-permute-start.47 = (bf16[160,1024]{1,0:T(8,128)(2,1)}, bf16[160,1024]{1,0:T(8,128)(2,1)}, u32[]{:S(2)}, u32[]{:S(2)}) collective-permute-start(bf16[160,1024]{1,0:T(8,128)(2,1)} %slice.1078), channel_id=1, source_target_pairs={{0,2},{1,3},{2,0},{3,1},{4,6},{5,7},{6,4},{7,5},{8,10},{9,11},{10,... | collective-permute-start | bytes 983048 | tf_op jit(solution)/shard_map/ppermute | solution.py:73
  573.7 9.8 %collective-permute-start.50 = (bf16[128,768]{0,1:T(8,128)(2,1)S(1)}, bf16[128,768]{0,1:T(8,128)(2,1)S(1)}, u32[]{:S(2)}, u32[]{:S(2)}) collective-permute-start(bf16[128,768]{0,1:T(8,128)(2,1)S(1)} %slice.1095), channel_id=1, source_target_pairs={{0,16},{4,20},{8,24},{12,28},{16,0},{20,4},{24,8},{28,12},{1,17},{... | collective-permute-start | bytes 589832 | tf_op jit(solution)/shard_map/ppermute | solution.py:73
  (221 other events, 1561.9 us)
